TPU v7x, 256 devices: a whole 4x4x8 slice. The times are simulated.
256 devices in a mesh: dp: 32 (over z, x), head: 8 (over y, core).
Axes of the slice: x: 4, y: 4, z: 8, core: 2. Of those that a mesh axis runs over, the one named last changes fastest.
Arguments:
- acts: bfloat16 [16384, 7168], P('dp', 'head'), may hold values from -18 to 18
- latent: bfloat16 [16384, 512], P('dp'), may hold values from -6 to 6
- kv_gain: bfloat16 [512], replicated, may hold values from 0.099609375 to 1.8984375
- up_weight: bfloat16 [64, 512, 256], P('head'), may hold values from -0.25 to 0.25
- kv_cot: bfloat16 [16384, 64, 256], P('dp', 'head'), may hold values from -1.5 to 1.5
- rope_grad: bfloat16 [16384, 64], P('dp'), may hold values from -6 to 6
Outputs:
- down_update: bfloat16 [7168, 576], P('head')
- up_update: bfloat16 [64, 512, 256], P('head')
- down_rms: float32 [], replicated
All inputs are finite; a program needn't handle non-finite values.
Results may differ from a plain program's by a relative error of at most 0.029.
Values may be sent and summed in bfloat16 or wider, within the bound.
A program may use at most 64 MiB of HBM per device.

v0:
```python
import math

import jax
import jax.numpy as jnp
from jax import lax
from jax.sharding import PartitionSpec as P

D = 7168
LAT = 512
NS_STEPS = 5


coef_a = 3.4445
coef_b = -4.775
coef_c = 2.0315
highest = lax.Precision.HIGHEST


def from_partner(block, axis, distance):
    count = lax.axis_size(axis)
    route = []
    for low in range(count):
        high = low | 1 << distance
        if high != low and high < count:
            route += [(low, high), (high, low)]
    return lax.ppermute(block, axis, route)


def orthogonalize(start, total_fn, scale):
    current = start
    for step in range(NS_STEPS):
        gram = total_fn(
            jnp.einsum("brk,brl->bkl", current, current, preferred_element_type=jnp.float32)
        )
        square = jnp.einsum("bkl,blm->bkm", gram, gram, precision=highest)
        mixer = coef_b * gram + coef_c * square
        wide = current.astype(jnp.float32)
        result = coef_a * wide + jnp.einsum("brk,bkl->brl", wide, mixer, precision=highest)
        if step == NS_STEPS - 1:
            return (scale * result).astype(jnp.bfloat16)
        current = result.astype(jnp.bfloat16)


def per_device(acts, latent, kv_gain, up_weight, kv_cot, rope_grad):
    lat32 = latent.astype(jnp.float32)
    gain32 = kv_gain.astype(jnp.float32)
    inv = lax.rsqrt(jnp.mean(lat32 * lat32, axis=1, keepdims=True) + 1e-06)
    normed = (lat32 * inv * gain32).astype(jnp.bfloat16)
    partial_cot = lax.dot_general(
        kv_cot, up_weight, (((1, 2), (0, 2)), ((), ())), preferred_element_type=jnp.float32
    )
    latent_cot = lax.psum(partial_cot, "head")
    scaled = latent_cot * gain32
    grad_latent = inv * scaled - lat32 * inv**3 * jnp.mean(lat32 * scaled, axis=1, keepdims=True)
    compressed = jnp.concatenate([grad_latent.astype(jnp.bfloat16), rope_grad], axis=1)
    down_shard = lax.psum_scatter(
        lax.dot_general(
            acts, compressed, (((0,), (0,)), ((), ())), preferred_element_type=jnp.float32
        ),
        "dp",
        scatter_dimension=0,
        tiled=True,
    )
    kdim = kv_cot.shape[2]
    up_full = jnp.einsum("tl,thk->hlk", normed, kv_cot, preferred_element_type=jnp.float32).reshape(
        -1, kdim
    )
    rows_up = up_full.shape[0] // lax.axis_size("dp")
    up_shard = lax.psum_scatter(up_full, "dp", scatter_dimension=0, tiled=True)
    down_total = lax.psum(jnp.sum(down_shard * down_shard), ("dp", "head"))
    token_count = acts.shape[0] * lax.axis_size("dp")
    down_rms = jnp.sqrt(down_total / float(token_count * D * compressed.shape[1]))
    down_start = (down_shard / (jnp.sqrt(down_total) + 1e-07)).astype(jnp.bfloat16)
    down_scale = 0.2 * math.sqrt(max(D, compressed.shape[1]))
    full_rows = lax.all_gather(down_start, "dp", axis=0, tiled=True)

    def total_head(gram):
        return lax.psum(gram, "head")

    down_update = orthogonalize(full_rows[None], total_head, down_scale)[0]
    count_heads = 1
    group_bits = (LAT // rows_up).bit_length() - 1

    def group_gram(value):
        for bit in range(group_bits):
            value = value + from_partner(value, "dp", bit)
        return value

    stacked = up_shard.reshape(count_heads, rows_up, kdim)
    first_gram = group_gram(jnp.einsum("brk,brl->bkl", stacked, stacked, precision=highest))
    squares = jnp.trace(first_gram, axis1=1, axis2=2)
    up_start = (stacked / (jnp.sqrt(squares)[:, None, None] + 1e-07)).astype(jnp.bfloat16)
    up_done = orthogonalize(up_start, group_gram, 0.2 * math.sqrt(max(LAT, kdim)))
    up_rows = lax.all_gather(up_done.reshape(rows_up, kdim), "dp", axis=0, tiled=True)
    up_update = up_rows.reshape(up_weight.shape)
    return (down_update, up_update, down_rms)


def solution(mesh):
    in_specs = (
        P("dp", "head"),
        P("dp", None),
        P(),
        P("head", None, None),
        P("dp", "head", None),
        P("dp", None),
    )
    out_specs = (P("head", None), P("head", None, None), P())
    return jax.shard_map(
        per_device, mesh=mesh, in_specs=in_specs, out_specs=out_specs, check_vma=False
    )
```

profile of v0, /device:TPU:8, one launch (start us, length us, event | category | flops | bytes accessed | tf_op | source)
XLA Modules:
  0.0 1093.7 jit_solution(8480838493061689577)
XLA Ops:
  12.8 68.2 %all-reduce.9.cloned.1.call-done = f32[512,512]{1,0:T(8,128)} async-done(((f32[512,512]{1,0:T(8,128)}), f32[512,512]{1,0:T(8,128)}) %all-reduce.9.cloned.1.call-update) | async-done | bytes 1048592 | tf_op jit(solution)/shard_map/psum | solution.py:52
  87.1 153.2 %all-reduce.21.cloned.1.call-done = f32[896,576]{0,1:T(8,128)} async-done(((f32[896,576]{0,1:T(8,128)}), f32[896,576]{0,1:T(8,128)}) %all-reduce.21.cloned.1.call-update) | async-done | bytes 2064400
  242.1 72.9 %psum.50 = f32[]{:T(128)} all-reduce(f32[]{:T(128)} %multiply_reduce_fusion), channel_id=1, replica_groups=mesh['dp'=32,'head'=8] {'dp','head'}, use_global_device_ids=true, to_apply=%region_5.0 | all-reduce | flops 1 | bytes 8 | tf_op jit(solution)/shard_map/psum | solution.py:70
  317.1 53.5 %all-gather = bf16[32,28,576]{2,1,0:T(8,128)(2,1)} all-gather(bf16[1,28,576]{2,1,0:T(8,128)(2,1)S(1)} %copy.21), channel_id=1, replica_groups=mesh['dp'=32,'head'=8] {'dp'}, dimensions={0}, use_global_device_ids=true | all-gather | bytes 1064448 | tf_op jit(solution)/shard_map/all_gather | solution.py:75
  375.1 5.1 fusion
  382.2 57.0 %all-reduce.11.cloned.1.call-done = f32[1,576,576]{2,1,0:T(8,128)} async-done(((f32[1,576,576]{2,1,0:T(8,128)}), f32[1,576,576]{2,1,0:T(8,128)}) %all-reduce.11.cloned.1.call-update) | async-done | bytes 1327120 | tf_op jit(solution)/shard_map/psum | solution.py:78
  439.2 6.2 fusion.17
  451.7 214.1 %reduce-scatter.3.cloned.1.call-done = f32[128,256]{1,0:T(8,128)} async-done(((f32[4096,256]{1,0:T(8,128)}), f32[128,256]{1,0:T(8,128)}) %reduce-scatter.3.cloned.1.call-update) | async-done | bytes 131088 | tf_op jit(solution)/shard_map/reduce_scatter | solution.py:69
  667.7 8.4 collective-permute-done
  678.5 55.1 %all-reduce.13.cloned.1.call-done = f32[1,576,576]{2,1,0:T(8,128)} async-done(((f32[1,576,576]{2,1,0:T(8,128)}), f32[1,576,576]{2,1,0:T(8,128)}) %all-reduce.13.cloned.1.call-update) | async-done | bytes 1327120 | tf_op jit(solution)/shard_map/psum | solution.py:78
  733.6 7.1 fusion.14
  744.7 4.8 add_convert_fusion.2
  760.1 5.5 collective-permute-done.4
  765.6 5.2 collective-permute-start.5
  770.8 52.9 %all-reduce.15.cloned.1.call-done = f32[1,576,576]{2,1,0:T(8,128)} async-done(((f32[1,576,576]{2,1,0:T(8,128)}), f32[1,576,576]{2,1,0:T(8,128)}) %all-reduce.15.cloned.1.call-update) | async-done | bytes 1327120 | tf_op jit(solution)/shard_map/psum | solution.py:78
  823.7 6.1 fusion.11
  847.9 63.4 %all-reduce.17.cloned.1.call-done = f32[1,576,576]{2,1,0:T(8,128)} async-done(((f32[1,576,576]{2,1,0:T(8,128)}), f32[1,576,576]{2,1,0:T(8,128)}) %all-reduce.17.cloned.1.call-update) | async-done | bytes 1327120 | tf_op jit(solution)/shard_map/psum | solution.py:78
  911.3 6.2 fusion.8
  932.9 4.0 collective-permute-start.11
  936.9 4.4 collective-permute-done.11
  943.2 57.2 %all-reduce.19.cloned.1.call-done = f32[1,576,576]{2,1,0:T(8,128)} async-done(((f32[1,576,576]{2,1,0:T(8,128)}), f32[1,576,576]{2,1,0:T(8,128)}) %all-reduce.19.cloned.1.call-update) | async-done | bytes 1327120 | tf_op jit(solution)/shard_map/psum | solution.py:78
  1000.4 6.1 fusion.5
  1006.6 4.0 multiply_convert_fusion
  1010.6 72.2 %all-gather.3.cloned.1.call-done = bf16[4096,256]{1,0:T(8,128)(2,1)} async-done(((bf16[128,256]{1,0:T(8,128)(2,1)}), bf16[4096,256]{1,0:T(8,128)(2,1)}) %all-gather.3.cloned.1.call-update) | async-done | bytes 2097168 | tf_op jit(solution)/shard_map/all_gather | solution.py:94
  (124 shorter events, 82.8 us)
Async XLA Ops:
  7.2 73.8 %all-reduce.9.cloned.1.call-start = ((), (), s32[]{:S(2)}) async-start(), calls=%async_computation.1 | async-start | bytes 2097152 | tf_op jit(solution)/shard_map/psum | solution.py:52
  12.6 68.4 %copy-start.2 = (bf16[512,512]{1,0:T(8,128)(2,1)S(1)}, bf16[512,512]{1,0:T(8,128)(2,1)}, u32[]{:S(2)}) copy-start(bf16[512,512]{1,0:T(8,128)(2,1)} %param.7) | copy-start | bytes 1572868
  12.6 227.6 %all-reduce.21.cloned.1.call-start = ((), (), s32[]{:S(2)}) async-start(), calls=%async_computation.9 | async-start | bytes 4128768
  85.2 354.0 %all-reduce.11.cloned.1.call-start = ((), (), s32[]{:S(2)}) async-start(), calls=%async_computation.2 | async-start | bytes 2949120 | tf_op jit(solution)/shard_map/psum | solution.py:78
  375.1 290.6 %reduce-scatter.3.cloned.1.call-start = ((), (), s32[]{:S(2)}) async-start(), calls=%async_computation.7 | async-start | bytes 4325376 | tf_op jit(solution)/shard_map/reduce_scatter | solution.py:69
  380.3 353.3 %all-reduce.13.cloned.1.call-start = ((), (), s32[]{:S(2)}) async-start(), calls=%async_computation.3 | async-start | bytes 2949120 | tf_op jit(solution)/shard_map/psum | solution.py:78
  451.6 372.1 %all-reduce.15.cloned.1.call-start = ((), (), s32[]{:S(2)}) async-start(), calls=%async_computation.4 | async-start | bytes 2949120 | tf_op jit(solution)/shard_map/psum | solution.py:78
  667.1 9.0 collective-permute-start
  676.1 66.8 %copy-start.10 = (f32[128,256]{1,0:T(8,128)S(1)}, f32[128,256]{1,0:T(8,128)}, u32[]{:S(2)}) copy-start(f32[128,256]{1,0:T(8,128)} %reduce-scatter.3.cloned.1.call-done) | copy-start | bytes 393220
  676.2 68.6 %copy-start.9 = (bf16[896,576]{0,1:T(8,128)(2,1)S(1)}, bf16[896,576]{0,1:T(8,128)(2,1)}, u32[]{:S(2)}) copy-start(bf16[896,576]{0,1:T(8,128)(2,1)} %copy-done.8) | copy-start | bytes 3096580
  676.2 64.5 %collective-permute-start.1 = (f32[1,256,256]{2,1,0:T(8,128)S(1)}, f32[1,256,256]{2,1,0:T(8,128)}, u32[]{:S(2)}, u32[]{:S(2)}) collective-permute-start(f32[1,256,256]{2,1,0:T(8,128)S(1)} %add.159), channel_id=1, source_target_pairs={{0,16},{16,0},{8,24},{24,8},{32,48},{48,32},{40,56},{56,40},{64,80... | collective-permute-start | bytes 786440 | tf_op jit(solution)/shard_map/ppermute | solution.py:26
  743.2 6.5 collective-permute-start.2
  749.7 8.0 collective-permute-start.3
  755.0 156.3 %all-reduce.17.cloned.1.call-start = ((), (), s32[]{:S(2)}) async-start(), calls=%async_computation.5 | async-start | bytes 2949120 | tf_op jit(solution)/shard_map/psum | solution.py:78
  758.5 7.1 collective-permute-start.4
  765.6 64.2 %collective-permute-start.5 = (f32[1,256,256]{2,1,0:T(8,128)S(1)}, f32[1,256,256]{2,1,0:T(8,128)S(1)}, u32[]{:S(2)}, u32[]{:S(2)}) collective-permute-start(f32[1,256,256]{2,1,0:T(8,128)S(1)} %add.166), channel_id=1, source_target_pairs={{0,16},{16,0},{8,24},{24,8},{32,48},{48,32},{40,56},{56,40},{64,80... | collective-permute-start | bytes 786440 | tf_op jit(solution)/shard_map/ppermute | solution.py:26
  830.8 6.5 collective-permute-start.6
  837.3 8.0 collective-permute-start.7
  842.6 157.8 %all-reduce.19.cloned.1.call-start = ((), (), s32[]{:S(2)}) async-start(), calls=%async_computation.6 | async-start | bytes 2949120 | tf_op jit(solution)/shard_map/psum | solution.py:78
  846.1 71.3 %collective-permute-start.8 = (f32[1,256,256]{2,1,0:T(8,128)S(1)}, f32[1,256,256]{2,1,0:T(8,128)S(1)}, u32[]{:S(2)}, u32[]{:S(2)}) collective-permute-start(f32[1,256,256]{2,1,0:T(8,128)S(1)} %convolution_bitcast_fusion.7), channel_id=1, source_target_pairs={{0,8},{8,0},{16,24},{24,16},{32,40},{40,32},{48,56},{56,48},{64,72... | collective-permute-start | bytes 786440 | tf_op jit(solution)/shard_map/ppermute | solution.py:26
  917.5 8.0 collective-permute-start.9
  926.4 6.5 collective-permute-start.10
  930.2 152.6 %all-gather.3.cloned.1.call-start = ((), (), s32[]{:S(2)}) async-start(), calls=%async_computation.8 | async-start | bytes 2162688 | tf_op jit(solution)/shard_map/all_gather | solution.py:94
  932.9 8.3 collective-permute-start.11
  (18 other events, 141.9 us)
Sparse Core Ops, SparseCore 0:
  12.8 68.2 all-reduce.8
  85.3 154.9 all-reduce.20
  375.2 63.9 all-reduce.10
  443.0 222.7 reduce-scatter.2
  668.7 64.8 all-reduce.12
  755.1 68.5 all-reduce.14
  842.7 68.5 all-reduce.16
  930.3 70.0 all-reduce.18
  1003.3 79.3 all-gather.2
where the time goes:
time: 1100 us; the launch traced here: 1090 us
  waiting for transfers between devices  823 us (75%)
  blocking collectives  126 us (11%)
  matrix products  78.2 us (7%)
  starting transfers between devices  29.8 us (3%)
  between operations  18.4 us (2%)
  local copies, waits for them, and re-layouts  11.1 us (1%)
    psum x5, waiting for transfers between devices, total_head(): return lax.psum(gram, 'head')  286 us
    reduce_scatter x1, waiting for transfers between devices, per_device(): up_shard = lax.psum_scatter(up_full, 'dp', scatter_dimension=0, tiled=True)  214 us
    unnamed x10, waiting for transfers between devices  153 us
    psum x1, blocking collectives, per_device(): down_total = lax.psum(jnp.sum(down_shard * down_shard), ('dp', 'head'))  72.9 us
    all_gather x1, waiting for transfers between devices, per_device(): lax.all_gather(up_done.reshape(rows_up, kdim), 'dp', axis=0, tiled=True)  72.2 us
    psum x1, waiting for transfers between devices, per_device(): latent_cot = lax.psum(partial_cot, 'head')  68.2 us
    all_gather x1, blocking collectives, per_device(): full_rows = lax.all_gather(down_start, 'dp', axis=0, tiled=True)  53.5 us
    dot_general x10, matrix products, orthogonalize(): square = jnp.einsum('bkl,blm->bkm', gram, gram, precision=highest)  33.7 us
  transfers between devices with their start and end apart: 21, of which 18 were waited for; matrix products, arithmetic and copies ran while one was open for 6% of the time, Pallas kernels for 0%

commit v1 on v0

v1 whole, which is shorter than its diff:
```python
import functools
import math

import jax
import jax.numpy as jnp
from jax import lax
from jax.experimental import pallas as pl
from jax.experimental.pallas import tpu as pltpu
from jax.sharding import PartitionSpec as P

MESH = pl.DeviceIdType.MESH
bf16 = jnp.bfloat16
f32 = jnp.float32

D = 7168
TOKENS = 16384
LAT = 512
ROPE = 64
COLS = LAT + ROPE
WIDE = 640
DH2 = 256
NX, NZ, NY, NC = 4, 8, 4, 2
TOK = 512
HALF = TOK // NC
QUART = HALF // NY
DLOC = 896
XROWS = DLOC // NX
ZROWS = 32
UROWS = LAT // NX

coef_a = 3.4445
coef_b = -4.775
coef_c = 2.0315

BLOCK_ROWS = [128, 128, 128, 128, 64]
PACK = []
at = 0
for bi in range(5):
    for bj in range(bi, 5):
        PACK.append((bi, bj, at, BLOCK_ROWS[bi]))
        at += BLOCK_ROWS[bi]
PACKED = at
GHALF = PACKED // NC
GQUART = GHALF // NY


def dot(a, b):
    return lax.dot_general(a, b, (((1,), (0,)), ((), ())), preferred_element_type=f32)


def dot_nt(a, b):
    return lax.dot_general(a, b, (((1,), (1,)), ((), ())), preferred_element_type=f32)


def split(value):
    high = value.astype(bf16)
    low = (value - high.astype(f32)).astype(bf16)
    return high, low


def dot3(a, b):
    return dot(a[0], b[0]) + dot(a[0], b[1]) + dot(a[1], b[0])


def eye(n):
    rows = lax.broadcasted_iota(jnp.int32, (n, n), 0)
    cols = lax.broadcasted_iota(jnp.int32, (n, n), 1)
    return rows == cols


def mixer_of(a_ref, parts, n):
    square = dot3(parts, parts)
    mixed = coef_b * a_ref[...] + coef_c * square
    return mixed + jnp.where(eye(n), coef_a, 0.0)


def newton_schulz(a_ref, q_ref, n):
    a = split(a_ref[...])
    m = mixer_of(a_ref, a, n)
    q_ref[...] = m
    m = split(m)
    a_ref[...] = dot3(split(dot3(a, m)), m)

    def body(_, carry):
        a = split(a_ref[...])
        m = split(mixer_of(a_ref, a, n))
        a_ref[...] = dot3(split(dot3(a, m)), m)
        q_ref[...] = dot3(split(q_ref[...]), m)
        return carry

    lax.fori_loop(0, 3, body, 0)
    m = split(mixer_of(a_ref, split(a_ref[...]), n))
    q_ref[...] = dot3(split(q_ref[...]), m)


def kernel(
    kv, w, acts, lat, gain, rope, down_out, up_out, rms_out,
    pcs, rcc, csum, ysend, yrecv, comp, acts_t, usend, uxr, uzs, uzr, u,
    dsend, dxr, zsend, zrecv, xrows, gpk, gcr, gsum, gyr, gfull, a_ref, q_ref, ua_ref, uq_ref,
    s_c, r_c, s_yr, r_yr, s_ya, r_ya, s_ca, r_ca,
    s_ux, r_ux, s_uz, r_uz, s_ua, r_ua, s_oz, r_oz, s_ox, r_ox,
    s_dx, r_dx, s_dz, r_dz, s_az, r_az, s_ax, r_ax,
    s_gc, r_gc, s_gr, r_gr, s_ga, r_ga, s_gb, r_gb,
):
    dp = lax.axis_index("dp")
    hd = lax.axis_index("head")
    z, x = dp // NX, dp % NX
    y, c = hd // NC, hd % NC

    def to_x(j):
        return (z * NX + (x + j) % NX, hd)

    def to_z(j):
        return (((z + j) % NZ) * NX + x, hd)

    def to_y(j):
        return (dp, ((y + j) % NY) * NC + c)

    other = (dp, y * NC + (1 - c))

    def send(src, dst, s, r, device):
        copy = pltpu.make_async_remote_copy(
            src_ref=src, dst_ref=dst, send_sem=s, recv_sem=r,
            device_id=device, device_id_type=MESH,
        )
        copy.start()
        return copy

    started = []

    def ds(start, size):
        return pl.ds(pl.multiple_of(start, size), size)

    barrier = pltpu.get_barrier_semaphore()
    peers = [other] + [to_y(j) for j in range(1, NY)]
    peers += [to_x(j) for j in range(1, NX)] + [to_z(j) for j in range(1, NZ)]
    for peer in peers:
        pl.semaphore_signal(barrier, inc=1, device_id=peer, device_id_type=MESH)

    def cot_rows(start):
        rows = ds(start, HALF)
        total = dot_nt(kv[rows, 0:DH2], w[0])
        for h in range(1, 8):
            total += dot_nt(kv[rows, h * DH2 : (h + 1) * DH2], w[h])
        return total

    pcs[...] = cot_rows((1 - c) * HALF).astype(bf16)
    pl.semaphore_wait(barrier, len(peers))
    first = send(pcs, rcc, s_c, r_c, other)
    started.append(first)
    csum[...] = cot_rows(c * HALF)
    first.wait_recv()
    csum[...] += rcc[...].astype(f32)
    ysend[...] = csum[...].astype(bf16)
    y_reduce = [
        send(ysend.at[ds(((y + j) % NY) * QUART, QUART)], yrecv.at[j - 1],
             s_yr.at[j - 1], r_yr.at[j - 1], to_y(j))
        for j in range(1, NY)
    ]
    started += y_reduce

    lat32 = lat[...].astype(f32)
    gain32 = gain[...].astype(f32)
    inv = lax.rsqrt(jnp.mean(lat32 * lat32, axis=1, keepdims=True) + 1e-06)
    normed_t = (lat32 * inv * gain32).T.astype(bf16)
    for h in range(8):
        cols = slice(h * DH2, (h + 1) * DH2)
        usend[:, cols] = dot(normed_t, kv[:, cols]).astype(bf16)
    u_x = [
        send(usend.at[ds(((x + j) % NX) * UROWS, UROWS)], uxr.at[j - 1],
             s_ux.at[j - 1], r_ux.at[j - 1], to_x(j))
        for j in range(1, NX)
    ]
    started += u_x

    total = csum[ds(y * QUART, QUART), :]
    for j in range(1, NY):
        y_reduce[j - 1].wait_recv()
        total += yrecv[j - 1].astype(f32)
    own = c * HALF + y * QUART
    lat_q = lat[ds(own, QUART), :].astype(f32)
    inv_q = lax.rsqrt(jnp.mean(lat_q * lat_q, axis=1, keepdims=True) + 1e-06)
    scaled = total * gain32
    grad = inv_q * scaled - lat_q * inv_q**3 * jnp.mean(lat_q * scaled, axis=1, keepdims=True)
    comp[ds(own, QUART), :] = grad.astype(bf16)
    mine = comp.at[ds(own, QUART)]
    y_all = [send(mine, mine, s_ya.at[j - 1], r_ya.at[j - 1], to_y(j)) for j in range(1, NY)]
    c_all = [send(mine, mine, s_ca.at[0], r_ca.at[0], other)]
    acts_t[...] = acts[...].T
    for j in range(1, NY):
        y_all[j - 1].wait_recv()
        piece = comp.at[ds(c * HALF + ((y - j + NY) % NY) * QUART, QUART)]
        c_all.append(send(piece, piece, s_ca.at[j], r_ca.at[j], other))
    started += y_all + c_all
    dsend[:, LAT:WIDE] = jnp.concatenate(
        [dot(acts_t[...], rope[...]).astype(bf16), jnp.zeros((DLOC, WIDE - COLS), bf16)], axis=1
    )
    for copy in c_all:
        copy.wait_recv()
    dsend[:, 0:LAT] = dot(acts_t[...], comp[...]).astype(bf16)
    d_x = [
        send(dsend.at[ds(((x + j) % NX) * XROWS, XROWS)], dxr.at[j - 1],
             s_dx.at[j - 1], r_dx.at[j - 1], to_x(j))
        for j in range(1, NX)
    ]
    started += d_x

    for copy in u_x:
        copy.wait_recv()
    for h in range(8):
        cols = slice(h * DH2, (h + 1) * DH2)
        part = usend[ds(x * UROWS, UROWS), cols].astype(f32)
        for j in range(NX - 1):
            part += uxr[j, :, cols].astype(f32)
        uzs[h] = part.astype(bf16)
    u_z = [
        send(uzs.at[(z + j) % NZ], uzr.at[j - 1], s_uz.at[j - 1], r_uz.at[j - 1], to_z(j))
        for j in range(1, NZ)
    ]
    started += u_z

    for copy in d_x:
        copy.wait_recv()
    part = dsend[ds(x * XROWS, XROWS), :].astype(f32)
    for j in range(NX - 1):
        part += dxr[j].astype(f32)
    zsend[0:XROWS, :] = part.astype(bf16)
    zsend[XROWS : NZ * ZROWS, :] = jnp.zeros((NZ * ZROWS - XROWS, WIDE), bf16)
    d_z = [
        send(zsend.at[ds(((z + j) % NZ) * ZROWS, ZROWS)], zrecv.at[j - 1],
             s_dz.at[j - 1], r_dz.at[j - 1], to_z(j))
        for j in range(1, NZ)
    ]
    started += d_z

    part = uzs[z].astype(f32)
    for j in range(1, NZ):
        u_z[j - 1].wait_recv()
        part += uzr[j - 1].astype(f32)
    u_mine = u.at[ds(x * UROWS, UROWS)]
    u[ds(x * UROWS, UROWS), :] = part.astype(bf16)
    u_all = [send(u_mine, u_mine, s_ua.at[j - 1], r_ua.at[j - 1], to_x(j)) for j in range(1, NX)]
    started += u_all

    part = zsend[ds(z * ZROWS, ZROWS), :].astype(f32)
    for j in range(1, NZ):
        d_z[j - 1].wait_recv()
        part += zrecv[j - 1].astype(f32)
    xrows[x, ds(z * ZROWS, ZROWS), :] = part.astype(bf16)
    z_mine = xrows.at[x, ds(z * ZROWS, ZROWS)]
    d_az = [send(z_mine, z_mine, s_az.at[j - 1], r_az.at[j - 1], to_z(j)) for j in range(1, NZ)]
    started += d_az

    for copy in u_all:
        copy.wait_recv()
    uval = u[...]
    ugram = dot(uval.astype(f32).T.astype(bf16), uval)
    usq = jnp.sum(jnp.where(eye(DH2), ugram, 0.0), keepdims=True)
    unorm = 1.0 / (jnp.sqrt(usq) + 1e-07)
    ua_ref[...] = ugram * unorm * unorm
    newton_schulz(ua_ref, uq_ref, DH2)

    for copy in d_az:
        copy.wait_recv()
    x_mine = xrows.at[x, pl.ds(0, XROWS)]
    d_ax = [send(x_mine, x_mine, s_ax.at[j - 1], r_ax.at[j - 1], to_x(j)) for j in range(1, NX)]
    started += d_ax

    uq = split(uq_ref[...] * (unorm * (0.2 * math.sqrt(LAT))))
    urow = u[ds(x * UROWS, UROWS), :]
    up_out[z, ds(x * UROWS, UROWS), :] = (dot(urow, uq[0]) + dot(urow, uq[1])).astype(bf16)
    o_mine = up_out.at[z, ds(x * UROWS, UROWS)]
    o_z = [send(o_mine, o_mine, s_oz.at[j - 1], r_oz.at[j - 1], to_z(j)) for j in range(1, NZ)]
    started += o_z

    for copy in d_ax:
        copy.wait_recv()
    rows_t = [xrows[i, 0:XROWS, :].astype(f32).T.astype(bf16) for i in range(NX)]
    for bi in range(5):
        size = BLOCK_ROWS[bi]
        row = sum(
            dot(rows_t[i][bi * 128 : bi * 128 + size, :], xrows[i, 0:XROWS, bi * 128 : WIDE])
            for i in range(NX)
        )
        for pi, pj, start, _ in PACK:
            if pi == bi:
                gpk[start : start + size, :] = row[:, (pj - bi) * 128 : (pj - bi + 1) * 128]
    g_c = send(gpk.at[ds((1 - c) * GHALF, GHALF)], gcr, s_gc, r_gc, other)
    started.append(g_c)
    g_c.wait_recv()
    gsum[...] = gpk[ds(c * GHALF, GHALF), :] + gcr[...]
    g_y = [
        send(gsum.at[ds(((y + j) % NY) * GQUART, GQUART)], gyr.at[j - 1],
             s_gr.at[j - 1], r_gr.at[j - 1], to_y(j))
        for j in range(1, NY)
    ]
    started += g_y

    for copy in o_z:
        copy.wait_recv()
    o_rows = up_out.at[:, ds(x * UROWS, UROWS)]
    o_x = [send(o_rows, o_rows, s_ox.at[j - 1], r_ox.at[j - 1], to_x(j)) for j in range(1, NX)]
    started += o_x

    part = gsum[ds(y * GQUART, GQUART), :]
    for j in range(1, NY):
        g_y[j - 1].wait_recv()
        part += gyr[j - 1]
    own = c * GHALF + y * GQUART
    gfull[ds(own, GQUART), :] = part
    g_mine = gfull.at[ds(own, GQUART)]
    g_all = [send(g_mine, g_mine, s_ga.at[j - 1], r_ga.at[j - 1], to_y(j)) for j in range(1, NY)]
    g_fwd = [send(g_mine, g_mine, s_gb.at[0], r_gb.at[0], other)]
    for j in range(1, NY):
        g_all[j - 1].wait_recv()
        piece = gfull.at[ds(c * GHALF + ((y - j + NY) % NY) * GQUART, GQUART)]
        g_fwd.append(send(piece, piece, s_gb.at[j], r_gb.at[j], other))
    started += g_all + g_fwd
    for copy in g_fwd:
        copy.wait_recv()

    sq = jnp.zeros((1, 1), f32)
    for bi, bj, start, size in PACK:
        if bi == bj:
            block = gfull[start : start + size, :]
            row_id = lax.broadcasted_iota(jnp.int32, block.shape, 0)
            col_id = lax.broadcasted_iota(jnp.int32, block.shape, 1)
            sq += jnp.sum(jnp.where(row_id == col_id, block, 0.0), keepdims=True)
    norm = 1.0 / (jnp.sqrt(sq) + 1e-07)
    for bi, bj, start, size in PACK:
        block = gfull[start : start + size, :] * norm * norm
        wide = BLOCK_ROWS[bj]
        a_ref[bi * 128 : bi * 128 + size, bj * 128 : bj * 128 + wide] = block[:, 0:wide]
        if bi != bj:
            a_ref[bj * 128 : bj * 128 + wide, bi * 128 : bi * 128 + size] = block.T[0:wide, :]
    rms_out[0] = jnp.sqrt(sq / float(TOKENS * D * COLS))[0, 0]
    newton_schulz(a_ref, q_ref, COLS)
    q = split(q_ref[...] * (norm * (0.2 * math.sqrt(D))))
    for i in range(NX):
        rows = xrows[i, 0:XROWS, 0:COLS]
        out = dot(rows, q[0]) + dot(rows, q[1])
        down_out[i * XROWS : (i + 1) * XROWS, :] = out.astype(bf16)
    for copy in o_x:
        copy.wait_recv()
    for copy in started:
        copy.wait_send()


def per_device(acts, latent, kv_gain, up_weight, kv_cot, rope_grad):
    vmem = pltpu.VMEM
    dma = lambda *n: pltpu.SemaphoreType.DMA(n)
    sems = lambda n: [dma(n), dma(n)]
    scratch = [
        vmem((HALF, LAT), bf16), vmem((HALF, LAT), bf16), vmem((HALF, LAT), f32),
        vmem((HALF, LAT), bf16), vmem((3, QUART, LAT), bf16), vmem((TOK, LAT), bf16),
        vmem((DLOC, TOK), bf16),
        vmem((LAT, 8 * DH2), bf16), vmem((3, UROWS, 8 * DH2), bf16), vmem((8, UROWS, DH2), bf16),
        vmem((7, UROWS, DH2), bf16), vmem((LAT, DH2), bf16),
        vmem((DLOC, WIDE), bf16), vmem((3, XROWS, WIDE), bf16), vmem((NZ * ZROWS, WIDE), bf16),
        vmem((7, ZROWS, WIDE), bf16), vmem((NX, NZ * ZROWS, WIDE), bf16),
        vmem((PACKED, 128), f32), vmem((GHALF, 128), f32), vmem((GHALF, 128), f32),
        vmem((3, GQUART, 128), f32), vmem((PACKED, 128), f32),
        vmem((COLS, COLS), f32), vmem((COLS, COLS), f32), vmem((DH2, DH2), f32), vmem((DH2, DH2), f32),
    ]
    one = pltpu.SemaphoreType.DMA
    scratch += [one, one] + sems(3) + sems(3) + sems(4)
    scratch += sems(3) + sems(7) + sems(3) + sems(7) + sems(3)
    scratch += sems(3) + sems(7) + sems(7) + sems(3)
    scratch += [one, one] + sems(3) + sems(3) + sems(4)
    in_vmem = pl.BlockSpec(memory_space=pltpu.VMEM)
    down, up, rms = pl.pallas_call(
        kernel,
        out_shape=(
            jax.ShapeDtypeStruct((DLOC, COLS), bf16),
            jax.ShapeDtypeStruct((8, LAT, DH2), bf16),
            jax.ShapeDtypeStruct((1,), f32),
        ),
        in_specs=[in_vmem] * 6,
        out_specs=(in_vmem, in_vmem, pl.BlockSpec(memory_space=pltpu.SMEM)),
        scratch_shapes=scratch,
        name="muon",
        compiler_params=pltpu.CompilerParams(
            collective_id=0, has_side_effects=True, vmem_limit_bytes=62 * 1024 * 1024
        ),
    )(kv_cot.reshape(TOK, 8 * DH2), up_weight, acts, latent, kv_gain.reshape(1, LAT), rope_grad)
    return down, up, rms.reshape(())


def solution(mesh):
    in_specs = (
        P("dp", "head"),
        P("dp", None),
        P(),
        P("head", None, None),
        P("dp", "head", None),
        P("dp", None),
    )
    out_specs = (P("head", None), P("head", None, None), P())
    return jax.shard_map(
        per_device, mesh=mesh, in_specs=in_specs, out_specs=out_specs, check_vma=False
    )
```

time: 1100 us -> 159 us (0.14)
  the two profiles are of different devices: /device:TPU:8 before, /device:TPU:5 now
where the time goes in v1:
time: 159 us
  Pallas kernels  146 us (92%)
  local copies, waits for them, and re-layouts  10.2 us (6%)
  between operations  2.41 us (2%)
    pallas_call x1, Pallas kernels, per_device(): pl.pallas_call(kernel, out_shape=(jax.ShapeDtypeStruct((DLOC, COLS), bf16...  146 us
    unnamed x6, local copies, waits for them, and re-layouts  8.99 us

profile of v1, /device:TPU:5, one launch (start us, length us, event | category | flops | bytes accessed | tf_op | source)
XLA Modules:
  0.0 158.8 jit_solution(4175045490223773556)
XLA Ops:
  0.6 1.2 reshape.16.gain
  1.9 1.6 %copy.9.rope = bf16[512,64]{1,0:T(8,128)(2,1)} copy(bf16[512,64]{0,1:T(8,128)(2,1)} %param.11) | data formatting | bytes 131072 | tf_op args[5]
  3.5 3.6 %copy.11 = bf16[64,8,8,256]{3,1,2,0:T(8,128)(2,1)} copy(bf16[64,8,8,256]{3,2,1,0:T(8,128)(2,1)} %bitcast.4) | data formatting | bytes 4194304
  7.0 146.2 %muon.1 = (bf16[896,576]{1,0:T(8,128)(2,1)}, bf16[8,512,256]{2,1,0:T(8,128)(2,1)}, f32[1]{0:T(128)}) custom-call(bf16[512,2048]{1,0:T(8,128)(2,1)} %bitcast.3, bf16[8,512,256]{2,1,0:T(8,128)(2,1)} %w.1, bf16[512,896]{1,0:T(8,128)(2,1)} %acts.1, bf16[512,512]{1,0:T(8,128)(2,1)} %lat.1, bf16[1,512]{1,0:T(2,128)(2,1)} %reshape.16.gain, bf16[512,64]{1,0:T(8,128)(2,1)} %copy.9.rope), custom_call_target="tpu_custom_call" | custom-call | tf_op jit(solution)/shard_map/muon/pallas_call | solution.py:371
  153.2 0.0 copy-start
  153.2 2.5 %copy.10 = bf16[896,576]{0,1:T(8,128)(2,1)} copy(bf16[896,576]{1,0:T(8,128)(2,1)} %get-tuple-element.9) | data formatting | bytes 2064384
  155.7 0.0 copy-done
  155.7 1.3 copy.14
Async XLA Ops:
  153.2 2.5 %copy-start = (bf16[8,512,256]{2,1,0:T(8,128)(2,1)S(1)}, bf16[8,512,256]{2,1,0:T(8,128)(2,1)}, u32[]{:S(2)}) copy-start(bf16[8,512,256]{2,1,0:T(8,128)(2,1)} %get-tuple-element.16) | copy-start | bytes 6291460

commit v2 on v1

v2 whole, which is shorter than its diff:
```python
import functools
import math

import jax
import jax.numpy as jnp
from jax import lax
from jax.experimental import pallas as pl
from jax.experimental.pallas import tpu as pltpu
from jax.sharding import PartitionSpec as P

MESH = pl.DeviceIdType.MESH
bf16 = jnp.bfloat16
f32 = jnp.float32

D = 7168
TOKENS = 16384
LAT = 512
ROPE = 64
COLS = LAT + ROPE
DH2 = 256
NX, NZ, NY, NC = 4, 8, 4, 2
TOK = 512
HALF = TOK // NC
QUART = HALF // NY
DLOC = 896
XROWS = DLOC // NX
ZROWS = 32
UROWS = LAT // NX

coef_a = 3.4445
coef_b = -4.775
coef_c = 2.0315

BLOCK_ROWS = [128, 128, 128, 128, 64]
PACK = []
at = 0
for bi in range(5):
    for bj in range(bi, 5):
        PACK.append((bi, bj, at, BLOCK_ROWS[bi]))
        at += BLOCK_ROWS[bi]
PACKED = at
GHALF = PACKED // NC
GQUART = GHALF // NY


def dot(a, b):
    return lax.dot_general(a, b, (((1,), (0,)), ((), ())), preferred_element_type=f32)


def dot_nt(a, b):
    return lax.dot_general(a, b, (((1,), (1,)), ((), ())), preferred_element_type=f32)


def split(value):
    high = value.astype(bf16)
    low = (value - high.astype(f32)).astype(bf16)
    return high, low


def eye(rows, cols):
    row_id = lax.broadcasted_iota(jnp.int32, (rows, cols), 0)
    col_id = lax.broadcasted_iota(jnp.int32, (rows, cols), 1)
    return row_id == col_id


class Small:
    def prepare(self, value):
        return split(value[0])

    def product(self, a, b):
        return (dot(a[0], b[0]) + dot(a[0], b[1]) + dot(a[1], b[0]),)

    def rough(self, a, b):
        return (dot(a[0], b[0]),)


class Large:
    def prepare(self, value):
        main, corner = value
        rest = jnp.concatenate([main[LAT:, :].T, corner], axis=0)
        return split(main), split(rest)

    def product(self, a, b):
        (main_h, main_l), (rest_h, rest_l) = a
        (cols_h, cols_l), (tail_h, tail_l) = b
        rest = jnp.concatenate([rest_h, rest_l, rest_h], axis=1)
        low_rows = jnp.concatenate([cols_h[LAT:], cols_h[LAT:], cols_l[LAT:]], axis=0)
        main = dot(main_h, cols_h[:LAT]) + dot(main_h, cols_l[:LAT]) + dot(main_l, cols_h[:LAT])
        main += dot(rest, low_rows)
        low_tail = jnp.concatenate([tail_h[LAT:], tail_h[LAT:], tail_l[LAT:]], axis=0)
        corner = dot(main_h[LAT:], tail_h[:LAT]) + dot(main_h[LAT:], tail_l[:LAT])
        corner += dot(main_l[LAT:], tail_h[:LAT]) + dot(rest[LAT:], low_tail)
        return main, corner

    def rough(self, a, b):
        main_h, rest_h = a[0][0], a[1][0]
        cols_h, tail_h = b[0][0], b[1][0]
        main = dot(main_h, cols_h[:LAT]) + dot(rest_h, cols_h[LAT:])
        corner = dot(main_h[LAT:], tail_h[:LAT]) + dot(rest_h[LAT:], tail_h[LAT:])
        return main, corner


class NewtonSchulz:
    def __init__(self, form, gram, mix):
        self.form, self.gram, self.mix = form, gram, mix

    def load(self, refs):
        return tuple(ref[...] for ref in refs)

    def store(self, refs, value):
        for ref, part in zip(refs, value):
            ref[...] = part

    def mixer(self, parts):
        square = self.form.product(parts, parts)
        out = []
        for ref, part in zip(self.gram, square):
            out.append(coef_b * ref[...] + coef_c * part + jnp.where(eye(*part.shape), coef_a, 0.0))
        return tuple(out)

    def advance(self, parts, mixed):
        half = self.form.prepare(self.form.product(parts, mixed))
        self.store(self.gram, self.form.product(half, mixed))

    def first(self):
        parts = self.form.prepare(self.load(self.gram))
        mixed = self.mixer(parts)
        self.store(self.mix, mixed)
        self.advance(parts, self.form.prepare(mixed))

    def middle(self, count):
        def body(_, carry):
            parts = self.form.prepare(self.load(self.gram))
            mixed = self.form.prepare(self.mixer(parts))
            self.advance(parts, mixed)
            mix = self.form.prepare(self.load(self.mix))
            self.store(self.mix, self.form.product(mix, mixed))
            return carry

        lax.fori_loop(0, count, body, 0)

    def last(self):
        parts = self.form.prepare(self.load(self.gram))
        mixed = self.form.prepare(self.mixer(parts))
        mix = self.form.prepare(self.load(self.mix))
        return self.form.rough(mix, mixed)


def kernel(
    kv, w, acts, lat, gain, rope, down_out, up_out, rms_out,
    pcs, rcc, csum, ysend, yrecv, comp, acts_t, usend, uxr, uzs, uzr, u,
    dsend, dxr, zsend, zrecv, zrows, xall, esend, exr, fsend, frecv, frows, eall,
    gpk, gcr, gsum, gyr, gfull, a_main, a_corner, q_main, q_corner, ua_ref, uq_ref,
    s_c, r_c, s_yr, r_yr, s_ya, r_ya, s_ca, r_ca,
    s_ux, r_ux, s_uz, r_uz, s_ua, r_ua, s_oz, r_oz, s_ow, r_ow, s_ox, r_ox,
    s_dx, r_dx, s_dz, r_dz, s_az, r_az, s_ax, r_ax,
    s_ex, r_ex, s_ez, r_ez, s_fz, r_fz, s_fx, r_fx,
    s_gc, r_gc, s_gr, r_gr, s_ga, r_ga, s_gb, r_gb,
):
    dp = lax.axis_index("dp")
    hd = lax.axis_index("head")
    z, x = dp // NX, dp % NX
    y, c = hd // NC, hd % NC

    def to_x(j):
        return (z * NX + (x + j) % NX, hd)

    def to_z(j):
        return (((z + j) % NZ) * NX + x, hd)

    def to_y(j):
        return (dp, ((y + j) % NY) * NC + c)

    other = (dp, y * NC + (1 - c))
    started = []

    def send(src, dst, s, r, device):
        copy = pltpu.make_async_remote_copy(
            src_ref=src, dst_ref=dst, send_sem=s, recv_sem=r,
            device_id=device, device_id_type=MESH,
        )
        copy.start()
        started.append(copy)
        return copy

    def ds(start, size):
        return pl.ds(pl.multiple_of(start, size), size)

    barrier = pltpu.get_barrier_semaphore()
    peers = [other] + [to_y(j) for j in range(1, NY)]
    peers += [to_x(j) for j in range(1, NX)] + [to_z(j) for j in range(1, NZ)]
    for peer in peers:
        pl.semaphore_signal(barrier, inc=1, device_id=peer, device_id_type=MESH)

    def scatter_x(src, dst, s, r):
        return [
            send(src.at[ds(((x + j) % NX) * XROWS, XROWS)], dst.at[j - 1], s.at[j - 1], r.at[j - 1], to_x(j))
            for j in range(1, NX)
        ]

    def sum_x(copies, src, dst):
        for copy in copies:
            copy.wait_recv()
        part = src[ds(x * XROWS, XROWS), :].astype(f32)
        for j in range(NX - 1):
            part += dst[j].astype(f32)
        return part

    def scatter_z(part, src, dst, s, r):
        src[0:XROWS, :] = part.astype(bf16)
        src[XROWS : NZ * ZROWS, :] = jnp.zeros((NZ * ZROWS - XROWS, src.shape[1]), bf16)
        return [
            send(src.at[ds(((z + j) % NZ) * ZROWS, ZROWS)], dst.at[j - 1], s.at[j - 1], r.at[j - 1], to_z(j))
            for j in range(1, NZ)
        ]

    def sum_z(copies, src, dst):
        part = src[ds(z * ZROWS, ZROWS), :].astype(f32)
        for j in range(1, NZ):
            copies[j - 1].wait_recv()
            part += dst[j - 1].astype(f32)
        return part

    def gather_z(part, rows, s, r):
        rows[ds(z * ZROWS, ZROWS), :] = part.astype(bf16)
        mine = rows.at[ds(z * ZROWS, ZROWS)]
        return [send(mine, mine, s.at[j - 1], r.at[j - 1], to_z(j)) for j in range(1, NZ)]

    def gather_x(copies, rows, every, s, r):
        for copy in copies:
            copy.wait_recv()
        block = ds(x * XROWS, XROWS)
        out = [
            send(rows.at[pl.ds(0, XROWS)], every.at[block], s.at[j - 1], r.at[j - 1], to_x(j))
            for j in range(1, NX)
        ]
        every[block, :] = rows[0:XROWS, :]
        return out

    def cot_rows(start):
        rows = ds(start, HALF)
        total = dot_nt(kv[rows, 0:DH2], w[0])
        for h in range(1, 8):
            total += dot_nt(kv[rows, h * DH2 : (h + 1) * DH2], w[h])
        return total

    pcs[...] = cot_rows((1 - c) * HALF).astype(bf16)
    pl.semaphore_wait(barrier, len(peers))
    first = send(pcs, rcc, s_c, r_c, other)
    csum[...] = cot_rows(c * HALF)
    acts_t[...] = acts[...].T
    esend[...] = jnp.concatenate(
        [dot_nt(acts_t[...], rope[...]).astype(bf16), jnp.zeros((DLOC, 128 - ROPE), bf16)], axis=1
    )
    e_x = scatter_x(esend, exr, s_ex, r_ex)
    first.wait_recv()
    csum[...] += rcc[...].astype(f32)
    ysend[...] = csum[...].astype(bf16)
    y_reduce = [
        send(ysend.at[ds(((y + j) % NY) * QUART, QUART)], yrecv.at[j - 1],
             s_yr.at[j - 1], r_yr.at[j - 1], to_y(j))
        for j in range(1, NY)
    ]
    lat32 = lat[...].astype(f32)
    gain32 = gain[...].astype(f32)
    inv = lax.rsqrt(jnp.mean(lat32 * lat32, axis=1, keepdims=True) + 1e-06)
    normed_t = (lat32 * inv * gain32).T.astype(bf16)
    for h in range(8):
        cols = slice(h * DH2, (h + 1) * DH2)
        usend[:, cols] = dot(normed_t, kv[:, cols]).astype(bf16)

    def up_x(j):
        return send(usend.at[ds(((x + j) % NX) * UROWS, UROWS)], uxr.at[j - 1],
                    s_ux.at[j - 1], r_ux.at[j - 1], to_x(j))

    u_x = [up_x(1), up_x(3)]
    e_z = scatter_z(sum_x(e_x, esend, exr), fsend, frecv, s_ez, r_ez)
    total = csum[ds(y * QUART, QUART), :]
    for j in range(1, NY):
        y_reduce[j - 1].wait_recv()
        total += yrecv[j - 1].astype(f32)
    own = c * HALF + y * QUART
    lat_q = lat[ds(own, QUART), :].astype(f32)
    inv_q = lax.rsqrt(jnp.mean(lat_q * lat_q, axis=1, keepdims=True) + 1e-06)
    scaled = total * gain32
    grad = inv_q * scaled - lat_q * inv_q**3 * jnp.mean(lat_q * scaled, axis=1, keepdims=True)
    comp[ds(own, QUART), :] = grad.astype(bf16)
    mine = comp.at[ds(own, QUART)]
    y_all = [send(mine, mine, s_ya.at[j - 1], r_ya.at[j - 1], to_y(j)) for j in range(1, NY)]
    c_all = [send(mine, mine, s_ca.at[0], r_ca.at[0], other)]
    e_az = gather_z(sum_z(e_z, fsend, frecv), frows, s_fz, r_fz)
    for j in range(1, NY):
        y_all[j - 1].wait_recv()
        piece = comp.at[ds(c * HALF + ((y - j + NY) % NY) * QUART, QUART)]
        c_all.append(send(piece, piece, s_ca.at[j], r_ca.at[j], other))
    for copy in c_all:
        copy.wait_recv()
    dsend[...] = dot(acts_t[...], comp[...]).astype(bf16)
    d_x = scatter_x(dsend, dxr, s_dx, r_dx)
    u_x.append(up_x(2))
    e_ax = gather_x(e_az, frows, eall, s_fx, r_fx)
    d_z = scatter_z(sum_x(d_x, dsend, dxr), zsend, zrecv, s_dz, r_dz)
    d_az = gather_z(sum_z(d_z, zsend, zrecv), zrows, s_az, r_az)
    for copy in u_x:
        copy.wait_recv()
    for h in range(8):
        cols = slice(h * DH2, (h + 1) * DH2)
        part = usend[ds(x * UROWS, UROWS), cols].astype(f32)
        for j in range(NX - 1):
            part += uxr[j, :, cols].astype(f32)
        uzs[h] = part.astype(bf16)
    d_ax = gather_x(d_az, zrows, xall, s_ax, r_ax)
    u_z = [
        send(uzs.at[(z + j) % NZ], uzr.at[j - 1], s_uz.at[j - 1], r_uz.at[j - 1], to_z(j))
        for j in range(1, NZ)
    ]
    for copy in d_ax + e_ax:
        copy.wait_recv()
    main_t = [xall[:, i * 128 : (i + 1) * 128].astype(f32).T.astype(bf16) for i in range(4)]
    tail_t = eall[...].astype(f32).T.astype(bf16)
    for bi in range(5):
        size = BLOCK_ROWS[bi]
        lhs = main_t[bi] if bi < 4 else tail_t[0:size, :]
        tail = dot(lhs, eall[...])
        main = dot(lhs, xall[:, bi * 128 : LAT]) if bi < 4 else None
        for pi, pj, start, _ in PACK:
            if pi == bi:
                gpk[start : start + size, :] = tail if pj == 4 else main[:, (pj - bi) * 128 : (pj - bi + 1) * 128]
    g_c = send(gpk.at[ds((1 - c) * GHALF, GHALF)], gcr, s_gc, r_gc, other)
    part = uzs[z].astype(f32)
    for j in range(1, NZ):
        u_z[j - 1].wait_recv()
        part += uzr[j - 1].astype(f32)
    u_mine = u.at[ds(x * UROWS, UROWS)]
    u[ds(x * UROWS, UROWS), :] = part.astype(bf16)
    u_all = [send(u_mine, u_mine, s_ua.at[j - 1], r_ua.at[j - 1], to_x(j)) for j in range(1, NX)]
    g_c.wait_recv()
    gsum[...] = gpk[ds(c * GHALF, GHALF), :] + gcr[...]
    g_y = [
        send(gsum.at[ds(((y + j) % NY) * GQUART, GQUART)], gyr.at[j - 1],
             s_gr.at[j - 1], r_gr.at[j - 1], to_y(j))
        for j in range(1, NY)
    ]
    for copy in u_all:
        copy.wait_recv()
    uval = u[...]
    ugram = dot(uval.astype(f32).T.astype(bf16), uval)
    usq = jnp.sum(jnp.where(eye(DH2, DH2), ugram, 0.0), keepdims=True)
    unorm = 1.0 / (jnp.sqrt(usq) + 1e-07)
    ua_ref[...] = ugram * unorm * unorm
    up_steps = NewtonSchulz(Small(), (ua_ref,), (uq_ref,))
    up_steps.first()
    part = gsum[ds(y * GQUART, GQUART), :]
    for j in range(1, NY):
        g_y[j - 1].wait_recv()
        part += gyr[j - 1]
    own = c * GHALF + y * GQUART
    gfull[ds(own, GQUART), :] = part
    g_mine = gfull.at[ds(own, GQUART)]
    g_all = [send(g_mine, g_mine, s_ga.at[j - 1], r_ga.at[j - 1], to_y(j)) for j in range(1, NY)]
    g_fwd = [send(g_mine, g_mine, s_gb.at[0], r_gb.at[0], other)]
    up_steps.middle(3)
    uq = (up_steps.last()[0] * (unorm * (0.2 * math.sqrt(LAT)))).astype(bf16)
    near, far = ds(x * UROWS, UROWS), ds(((x + 2) % NX) * UROWS, UROWS)
    up_out[z, near, :] = dot(u[near, :], uq).astype(bf16)
    up_out[z, far, :] = dot(u[far, :], uq).astype(bf16)
    o_near, o_far = up_out.at[z, near], up_out.at[z, far]
    o_z = [send(o_near, o_near, s_oz.at[j - 1], r_oz.at[j - 1], to_z(j)) for j in range(1, NZ)]
    o_w = [send(o_far, o_far, s_ow.at[j - 1], r_ow.at[j - 1], to_z(j)) for j in range(1, NZ)]
    for j in range(1, NY):
        g_all[j - 1].wait_recv()
        piece = gfull.at[ds(c * GHALF + ((y - j + NY) % NY) * GQUART, GQUART)]
        g_fwd.append(send(piece, piece, s_gb.at[j], r_gb.at[j], other))
    for copy in g_fwd:
        copy.wait_recv()
    sq = jnp.zeros((1, 1), f32)
    for bi, bj, start, size in PACK:
        if bi == bj:
            block = gfull[start : start + size, :]
            sq += jnp.sum(jnp.where(eye(size, 128), block, 0.0), keepdims=True)
    norm = 1.0 / (jnp.sqrt(sq) + 1e-07)
    rms_out[0] = jnp.sqrt(sq / float(TOKENS * D * COLS))[0, 0]
    for bi, bj, start, size in PACK:
        block = gfull[start : start + size, :] * norm * norm
        rows = slice(bi * 128, bi * 128 + size)
        if bj < 4:
            a_main[rows, bj * 128 : (bj + 1) * 128] = block
        elif bi == 4:
            a_corner[...] = block[:, 0:ROPE]
        if bi != bj:
            wide = BLOCK_ROWS[bj]
            a_main[bj * 128 : bj * 128 + wide, rows] = block.T[0:wide, :]
    steps = NewtonSchulz(Large(), (a_main, a_corner), (q_main, q_corner))
    steps.first()
    for copy in o_z:
        copy.wait_recv()
    o_rows = up_out.at[:, near]
    o_x = [send(o_rows, o_rows, s_ox.at[i], r_ox.at[i], to_x(j)) for i, j in enumerate((1, 3))]
    steps.middle(3)
    main, corner = steps.last()
    scale = norm * (0.2 * math.sqrt(D))
    main = (main * scale).astype(bf16)
    rest = main[LAT:, :]
    corner = (corner * scale).astype(bf16)
    down_out[0:LAT, :] = (dot_nt(main[0:LAT], xall[...]) + dot(main[LAT:].astype(f32).T.astype(bf16), tail_t[0:ROPE])).astype(bf16)
    down_out[LAT:, :] = (dot_nt(rest, xall[...]) + dot(corner, tail_t[0:ROPE])).astype(bf16)
    for copy in o_w + o_x:
        copy.wait_recv()
    for copy in started:
        copy.wait_send()


def per_device(acts, latent, kv_gain, up_weight, kv_cot, rope_grad):
    vmem = pltpu.VMEM
    one = pltpu.SemaphoreType.DMA
    sems = lambda n: [pltpu.SemaphoreType.DMA((n,)), pltpu.SemaphoreType.DMA((n,))]

    def rows_of(width):
        return [
            vmem((DLOC, width), bf16), vmem((3, XROWS, width), bf16), vmem((NZ * ZROWS, width), bf16),
            vmem((7, ZROWS, width), bf16), vmem((NZ * ZROWS, width), bf16), vmem((DLOC, width), bf16),
        ]

    scratch = [
        vmem((HALF, LAT), bf16), vmem((HALF, LAT), bf16), vmem((HALF, LAT), f32),
        vmem((HALF, LAT), bf16), vmem((3, QUART, LAT), bf16), vmem((TOK, LAT), bf16),
        vmem((DLOC, TOK), bf16),
        vmem((LAT, 8 * DH2), bf16), vmem((3, UROWS, 8 * DH2), bf16), vmem((8, UROWS, DH2), bf16),
        vmem((7, UROWS, DH2), bf16), vmem((LAT, DH2), bf16),
    ]
    scratch += rows_of(LAT) + rows_of(128)
    scratch += [
        vmem((PACKED, 128), f32), vmem((GHALF, 128), f32), vmem((GHALF, 128), f32),
        vmem((3, GQUART, 128), f32), vmem((PACKED, 128), f32),
        vmem((COLS, LAT), f32), vmem((ROPE, ROPE), f32), vmem((COLS, LAT), f32), vmem((ROPE, ROPE), f32),
        vmem((DH2, DH2), f32), vmem((DH2, DH2), f32),
    ]
    scratch += [one, one] + sems(3) + sems(3) + sems(4)
    scratch += sems(3) + sems(7) + sems(3) + sems(7) + sems(7) + sems(2)
    scratch += sems(3) + sems(7) + sems(7) + sems(3)
    scratch += sems(3) + sems(7) + sems(7) + sems(3)
    scratch += [one, one] + sems(3) + sems(3) + sems(4)
    in_vmem = pl.BlockSpec(memory_space=pltpu.VMEM)
    down, up, rms = pl.pallas_call(
        kernel,
        out_shape=(
            jax.ShapeDtypeStruct((COLS, DLOC), bf16),
            jax.ShapeDtypeStruct((8, LAT, DH2), bf16),
            jax.ShapeDtypeStruct((1,), f32),
        ),
        in_specs=[in_vmem] * 6,
        out_specs=(in_vmem, in_vmem, pl.BlockSpec(memory_space=pltpu.SMEM)),
        scratch_shapes=scratch,
        name="muon",
        compiler_params=pltpu.CompilerParams(
            collective_id=0, has_side_effects=True, vmem_limit_bytes=62 * 1024 * 1024
        ),
    )(kv_cot.reshape(TOK, 8 * DH2), up_weight, acts, latent, kv_gain.reshape(1, LAT), rope_grad.T)
    return down.T, up, rms.reshape(())


def solution(mesh):
    in_specs = (
        P("dp", "head"),
        P("dp", None),
        P(),
        P("head", None, None),
        P("dp", "head", None),
        P("dp", None),
    )
    out_specs = (P("head", None), P("head", None, None), P())
    return jax.shard_map(
        per_device, mesh=mesh, in_specs=in_specs, out_specs=out_specs, check_vma=False
    )
```

time: 159 us -> 139 us (0.87)
  the two profiles are of different devices: /device:TPU:5 before, /device:TPU:8 now
where the time goes in v2:
time: 139 us; the launch traced here: 137 us
  Pallas kernels  124 us (89%)
  local copies, waits for them, and re-layouts  10.2 us (7%)
  between operations  2.31 us (2%)
    pallas_call x1, Pallas kernels, per_device(): pl.pallas_call(kernel, out_shape=(jax.ShapeDtypeStruct((COLS, DLOC), bf16...  124 us
    unnamed x3, local copies, waits for them, and re-layouts  8.9 us

profile of v2, /device:TPU:8, one launch (start us, length us, event | category | flops | bytes accessed | tf_op | source)
XLA Modules:
  0.0 136.6 jit_solution(1087673597564781938)
XLA Ops:
  0.6 1.3 reshape.16.gain
  1.9 3.6 %copy.9 = bf16[64,8,8,256]{3,1,2,0:T(8,128)(2,1)} copy(bf16[64,8,8,256]{3,2,1,0:T(8,128)(2,1)} %bitcast.6) | data formatting | bytes 4194304
  5.5 124.1 %muon.1 = (bf16[576,896]{1,0:T(8,128)(2,1)}, bf16[8,512,256]{2,1,0:T(8,128)(2,1)}, f32[1]{0:T(128)}) custom-call(bf16[512,2048]{1,0:T(8,128)(2,1)} %bitcast.5, bf16[8,512,256]{2,1,0:T(8,128)(2,1)} %w.1, bf16[512,896]{1,0:T(8,128)(2,1)} %acts.1, bf16[512,512]{1,0:T(8,128)(2,1)} %lat.1, bf16[1,512]{1,0:T(2,128)(2,1)} %reshape.16.gain, bf16[64,512]{1,0:T(8,128)(2,1)} %bitcast.8), custom_call_target="tpu_custom_call" | custom-call | tf_op jit(solution)/shard_map/muon/pallas_call | solution.py:444
  129.6 2.3 %copy.13 = bf16[896,576]{0,1:T(8,128)(2,1)} copy(bf16[896,576]{0,1:T(8,128)(2,1)} %bitcast.7) | data formatting | bytes 2064384
  131.9 3.0 %copy.14 = bf16[8,512,256]{2,1,0:T(8,128)(2,1)} copy(bf16[8,512,256]{2,1,0:T(8,128)(2,1)} %get-tuple-element.13) | data formatting | bytes 4194304

commit v3 on v2

--- a/solution.py
+++ b/solution.py
@@ -26,6 +26,13 @@
 XROWS = DLOC // NX
 ZROWS = 32
 UROWS = LAT // NX
+AROWS, BROWS = 512, 384
+AX, AZ = AROWS // NX, AROWS // (NX * NZ)
+BZ, BX = BROWS // NZ, 16
+UA, UB = 384, 128
+UAX, UBX = UA // NX, UB // NX
+
+VMEM_LIMIT = 40 * 1024 * 1024
 
 coef_a = 3.4445
 coef_b = -4.775
@@ -147,13 +154,14 @@
 
 
 def kernel(
-    kv, w, acts, lat, gain, rope, down_out, up_out, rms_out,
-    pcs, rcc, csum, ysend, yrecv, comp, acts_t, usend, uxr, uzs, uzr, u,
-    dsend, dxr, zsend, zrecv, zrows, xall, esend, exr, fsend, frecv, frows, eall,
+    kv, w, acts, lat, gain, rope, up_out, rms_out, xall, eall, qm_out, qc_out,
+    pcs, rcc, csum, ysend, yrecv, comp, acts_t, usend, uxr, uzs, uzr, vzr, vxs, vxr, u,
+    dsend, axr, azs, azr, bzr, bxs, bxr, brow, esend, exr, fsend, frecv, frows,
     gpk, gcr, gsum, gyr, gfull, a_main, a_corner, q_main, q_corner, ua_ref, uq_ref,
     s_c, r_c, s_yr, r_yr, s_ya, r_ya, s_ca, r_ca,
-    s_ux, r_ux, s_uz, r_uz, s_ua, r_ua, s_oz, r_oz, s_ow, r_ow, s_ox, r_ox,
-    s_dx, r_dx, s_dz, r_dz, s_az, r_az, s_ax, r_ax,
+    s_ux, r_ux, s_uz, r_uz, s_vz, r_vz, s_vx, r_vx, s_ua, r_ua, s_ub, r_ub, s_oz, r_oz, s_ow, r_ow, s_ox, r_ox,
+    s_ax, r_ax, s_az, r_az, s_bz, r_bz, s_bx, r_bx,
+    s_gaz, r_gaz, s_gax, r_gax, s_gbx, r_gbx, s_gbz, r_gbz,
     s_ex, r_ex, s_ez, r_ez, s_fz, r_fz, s_fx, r_fx,
     s_gc, r_gc, s_gr, r_gr, s_ga, r_ga, s_gb, r_gb,
 ):
@@ -183,8 +191,20 @@
         started.append(copy)
         return copy
 
-    def ds(start, size):
-        return pl.ds(pl.multiple_of(start, size), size)
+    def ds(start, size, unit=None):
+        return pl.ds(pl.multiple_of(start, unit or size), size)
+
+    def to_all_x(src, dst, s, r):
+        return [send(src(j), dst(j), s.at[j - 1], r.at[j - 1], to_x(j)) for j in range(1, NX)]
+
+    def to_all_z(src, dst, s, r):
+        return [send(src(j), dst(j), s.at[j - 1], r.at[j - 1], to_z(j)) for j in range(1, NZ)]
+
+    def received(copies, total, slots):
+        for i, copy in enumerate(copies):
+            copy.wait_recv()
+            total += slots[i].astype(f32)
+        return total
 
     barrier = pltpu.get_barrier_semaphore()
     peers = [other] + [to_y(j) for j in range(1, NY)]
@@ -262,18 +282,17 @@
         for j in range(1, NY)
     ]
     lat32 = lat[...].astype(f32)
-    gain32 = gain[...].astype(f32)
+    gain32 = gain[...].astype(f32).reshape(1, LAT)
     inv = lax.rsqrt(jnp.mean(lat32 * lat32, axis=1, keepdims=True) + 1e-06)
     normed_t = (lat32 * inv * gain32).T.astype(bf16)
     for h in range(8):
         cols = slice(h * DH2, (h + 1) * DH2)
         usend[:, cols] = dot(normed_t, kv[:, cols]).astype(bf16)
 
-    def up_x(j):
-        return send(usend.at[ds(((x + j) % NX) * UROWS, UROWS)], uxr.at[j - 1],
-                    s_ux.at[j - 1], r_ux.at[j - 1], to_x(j))
-
-    u_x = [up_x(1), up_x(3)]
+    u_x = to_all_x(lambda j: usend.at[ds(((x + j) % NX) * UAX, UAX)], lambda j: uxr.at[j - 1], s_ux, r_ux)
+    v_z = to_all_z(
+        lambda j: usend.at[pl.ds(UA, UB), ds(((z + j) % NZ) * DH2, DH2)], lambda j: vzr.at[j - 1], s_vz, r_vz
+    )
     e_z = scatter_z(sum_x(e_x, esend, exr), fsend, frecv, s_ez, r_ez)
     total = csum[ds(y * QUART, QUART), :]
     for j in range(1, NY):
@@ -295,26 +314,50 @@
         c_all.append(send(piece, piece, s_ca.at[j], r_ca.at[j], other))
     for copy in c_all:
         copy.wait_recv()
-    dsend[...] = dot(acts_t[...], comp[...]).astype(bf16)
-    d_x = scatter_x(dsend, dxr, s_dx, r_dx)
-    u_x.append(up_x(2))
+    dsend[AROWS:, :] = dot(acts_t[AROWS:, :], comp[...]).astype(bf16)
+    b_z = to_all_z(
+        lambda j: dsend.at[ds(AROWS + ((z + j) % NZ) * BZ, BZ, 16)], lambda j: bzr.at[j - 1], s_bz, r_bz
+    )
+    dsend[0:AROWS, :] = dot(acts_t[0:AROWS, :], comp[...]).astype(bf16)
+    a_x = to_all_x(lambda j: dsend.at[ds(((x + j) % NX) * AX, AX)], lambda j: axr.at[j - 1], s_ax, r_ax)
     e_ax = gather_x(e_az, frows, eall, s_fx, r_fx)
-    d_z = scatter_z(sum_x(d_x, dsend, dxr), zsend, zrecv, s_dz, r_dz)
-    d_az = gather_z(sum_z(d_z, zsend, zrecv), zrows, s_az, r_az)
+    part = received(v_z, usend[UA:, ds(z * DH2, DH2)].astype(f32), vzr)
+    vxs[...] = part.astype(bf16)
+    v_x = to_all_x(lambda j: vxs.at[ds(((x + j) % NX) * UBX, UBX)], lambda j: vxr.at[j - 1], s_vx, r_vx)
+    azs[...] = received(a_x, dsend[ds(x * AX, AX), :].astype(f32), axr).astype(bf16)
+    a_z = to_all_z(lambda j: azs.at[ds(((z + j) % NZ) * AZ, AZ)], lambda j: azr.at[j - 1], s_az, r_az)
+    part = received(b_z, dsend[ds(AROWS + z * BZ, BZ, 16), :].astype(f32), bzr)
+    bxs[0:BZ, :] = part.astype(bf16)
+    bxs[BZ:, :] = jnp.zeros((NX * BX - BZ, LAT), bf16)
+    b_x = to_all_x(lambda j: bxs.at[ds(((x + j) % NX) * BX, BX)], lambda j: bxr.at[j - 1], s_bx, r_bx)
+    own = ds(x * AX + z * AZ, AZ)
+    xall[own, :] = received(a_z, azs[ds(z * AZ, AZ), :].astype(f32), azr).astype(bf16)
+    mine = xall.at[own]
+    g_az = to_all_z(lambda j: mine, lambda j: mine, s_gaz, r_gaz)
+    own_b = ds(x * BX, BX)
+    brow[own_b, :] = received(b_x, bxs[own_b, :].astype(f32), bxr).astype(bf16)
+    mine_b = brow.at[own_b]
+    g_bx = to_all_x(lambda j: mine_b, lambda j: mine_b, s_gbx, r_gbx)
+    for copy in g_bx:
+        copy.wait_recv()
+    own_z = ds(AROWS + z * BZ, BZ, 16)
+    xall[own_z, :] = brow[0:BZ, :]
+    mine_z = xall.at[own_z]
+    g_bz = to_all_z(lambda j: mine_z, lambda j: mine_z, s_gbz, r_gbz)
+    for copy in g_az:
+        copy.wait_recv()
+    mine_x = xall.at[ds(x * AX, AX)]
+    g_ax = to_all_x(lambda j: mine_x, lambda j: mine_x, s_gax, r_gax)
     for copy in u_x:
         copy.wait_recv()
     for h in range(8):
         cols = slice(h * DH2, (h + 1) * DH2)
-        part = usend[ds(x * UROWS, UROWS), cols].astype(f32)
+        part = usend[ds(x * UAX, UAX), cols].astype(f32)
         for j in range(NX - 1):
             part += uxr[j, :, cols].astype(f32)
         uzs[h] = part.astype(bf16)
-    d_ax = gather_x(d_az, zrows, xall, s_ax, r_ax)
-    u_z = [
-        send(uzs.at[(z + j) % NZ], uzr.at[j - 1], s_uz.at[j - 1], r_uz.at[j - 1], to_z(j))
-        for j in range(1, NZ)
-    ]
-    for copy in d_ax + e_ax:
+    u_z = to_all_z(lambda j: uzs.at[(z + j) % NZ], lambda j: uzr.at[j - 1], s_uz, r_uz)
+    for copy in g_ax + g_bz + e_ax:
         copy.wait_recv()
     main_t = [xall[:, i * 128 : (i + 1) * 128].astype(f32).T.astype(bf16) for i in range(4)]
     tail_t = eall[...].astype(f32).T.astype(bf16)
@@ -327,13 +370,6 @@
             if pi == bi:
                 gpk[start : start + size, :] = tail if pj == 4 else main[:, (pj - bi) * 128 : (pj - bi + 1) * 128]
     g_c = send(gpk.at[ds((1 - c) * GHALF, GHALF)], gcr, s_gc, r_gc, other)
-    part = uzs[z].astype(f32)
-    for j in range(1, NZ):
-        u_z[j - 1].wait_recv()
-        part += uzr[j - 1].astype(f32)
-    u_mine = u.at[ds(x * UROWS, UROWS)]
-    u[ds(x * UROWS, UROWS), :] = part.astype(bf16)
-    u_all = [send(u_mine, u_mine, s_ua.at[j - 1], r_ua.at[j - 1], to_x(j)) for j in range(1, NX)]
     g_c.wait_recv()
     gsum[...] = gpk[ds(c * GHALF, GHALF), :] + gcr[...]
     g_y = [
@@ -341,7 +377,12 @@
              s_gr.at[j - 1], r_gr.at[j - 1], to_y(j))
         for j in range(1, NY)
     ]
-    for copy in u_all:
+    rows_a, rows_b = ds(x * UAX, UAX), ds(UA + x * UBX, UBX)
+    u[rows_b, :] = received(v_x, vxs[ds(x * UBX, UBX), :].astype(f32), vxr).astype(bf16)
+    u_b = to_all_x(lambda j: u.at[rows_b], lambda j: u.at[rows_b], s_ub, r_ub)
+    u[rows_a, :] = received(u_z, uzs[z].astype(f32), uzr).astype(bf16)
+    u_a = to_all_x(lambda j: u.at[rows_a], lambda j: u.at[rows_a], s_ua, r_ua)
+    for copy in u_a + u_b:
         copy.wait_recv()
     uval = u[...]
     ugram = dot(uval.astype(f32).T.astype(bf16), uval)
@@ -399,15 +440,22 @@
     steps.middle(3)
     main, corner = steps.last()
     scale = norm * (0.2 * math.sqrt(D))
-    main = (main * scale).astype(bf16)
-    rest = main[LAT:, :]
-    corner = (corner * scale).astype(bf16)
-    down_out[0:LAT, :] = (dot_nt(main[0:LAT], xall[...]) + dot(main[LAT:].astype(f32).T.astype(bf16), tail_t[0:ROPE])).astype(bf16)
-    down_out[LAT:, :] = (dot_nt(rest, xall[...]) + dot(corner, tail_t[0:ROPE])).astype(bf16)
+    qm_out[...] = (main * scale).astype(bf16)
+    qc_out[...] = (corner * scale).astype(bf16)
     for copy in o_w + o_x:
         copy.wait_recv()
     for copy in started:
         copy.wait_send()
+
+
+def finish(qm, qc, xall, eall, up, down_out, up_out, sem):
+    store = pltpu.make_async_copy(up, up_out, sem)
+    store.start()
+    tail = eall[:, 0:ROPE]
+    side = qm[LAT:, :].astype(f32).T.astype(bf16)
+    down_out[0:LAT, :] = (dot_nt(qm[0:LAT, :], xall[...]) + dot_nt(side, tail)).astype(bf16)
+    down_out[LAT:, :] = (dot_nt(qm[LAT:, :], xall[...]) + dot_nt(qc[...], tail)).astype(bf16)
+    store.wait()
 
 
 def per_device(acts, latent, kv_gain, up_weight, kv_cot, rope_grad):
@@ -415,47 +463,53 @@
     one = pltpu.SemaphoreType.DMA
     sems = lambda n: [pltpu.SemaphoreType.DMA((n,)), pltpu.SemaphoreType.DMA((n,))]
 
-    def rows_of(width):
-        return [
-            vmem((DLOC, width), bf16), vmem((3, XROWS, width), bf16), vmem((NZ * ZROWS, width), bf16),
-            vmem((7, ZROWS, width), bf16), vmem((NZ * ZROWS, width), bf16), vmem((DLOC, width), bf16),
-        ]
-
     scratch = [
         vmem((HALF, LAT), bf16), vmem((HALF, LAT), bf16), vmem((HALF, LAT), f32),
         vmem((HALF, LAT), bf16), vmem((3, QUART, LAT), bf16), vmem((TOK, LAT), bf16),
         vmem((DLOC, TOK), bf16),
-        vmem((LAT, 8 * DH2), bf16), vmem((3, UROWS, 8 * DH2), bf16), vmem((8, UROWS, DH2), bf16),
-        vmem((7, UROWS, DH2), bf16), vmem((LAT, DH2), bf16),
-    ]
-    scratch += rows_of(LAT) + rows_of(128)
-    scratch += [
+        vmem((LAT, 8 * DH2), bf16), vmem((3, UAX, 8 * DH2), bf16), vmem((8, UAX, DH2), bf16),
+        vmem((7, UAX, DH2), bf16), vmem((7, UB, DH2), bf16), vmem((UB, DH2), bf16),
+        vmem((3, UBX, DH2), bf16), vmem((LAT, DH2), bf16),
+        vmem((DLOC, LAT), bf16), vmem((3, AX, LAT), bf16), vmem((AX, LAT), bf16), vmem((7, AZ, LAT), bf16),
+        vmem((7, BZ, LAT), bf16), vmem((NX * BX, LAT), bf16), vmem((3, BX, LAT), bf16),
+        vmem((NX * BX, LAT), bf16),
+        vmem((DLOC, 128), bf16), vmem((3, XROWS, 128), bf16), vmem((NZ * ZROWS, 128), bf16),
+        vmem((7, ZROWS, 128), bf16), vmem((NZ * ZROWS, 128), bf16),
         vmem((PACKED, 128), f32), vmem((GHALF, 128), f32), vmem((GHALF, 128), f32),
         vmem((3, GQUART, 128), f32), vmem((PACKED, 128), f32),
         vmem((COLS, LAT), f32), vmem((ROPE, ROPE), f32), vmem((COLS, LAT), f32), vmem((ROPE, ROPE), f32),
         vmem((DH2, DH2), f32), vmem((DH2, DH2), f32),
     ]
     scratch += [one, one] + sems(3) + sems(3) + sems(4)
-    scratch += sems(3) + sems(7) + sems(3) + sems(7) + sems(7) + sems(2)
-    scratch += sems(3) + sems(7) + sems(7) + sems(3)
+    scratch += sems(3) + sems(7) + sems(7) + sems(3) + sems(3) + sems(3) + sems(7) + sems(7) + sems(2)
+    scratch += sems(3) + sems(7) + sems(7) + sems(3) + sems(7) + sems(3) + sems(3) + sems(7)
     scratch += sems(3) + sems(7) + sems(7) + sems(3)
     scratch += [one, one] + sems(3) + sems(3) + sems(4)
     in_vmem = pl.BlockSpec(memory_space=pltpu.VMEM)
-    down, up, rms = pl.pallas_call(
+    shape = jax.ShapeDtypeStruct
+    up, rms, xall, eall, qm, qc = pl.pallas_call(
         kernel,
         out_shape=(
-            jax.ShapeDtypeStruct((COLS, DLOC), bf16),
-            jax.ShapeDtypeStruct((8, LAT, DH2), bf16),
-            jax.ShapeDtypeStruct((1,), f32),
+            shape((8, LAT, DH2), bf16), shape((1,), f32), shape((DLOC, LAT), bf16), shape((DLOC, 128), bf16),
+            shape((COLS, LAT), bf16), shape((ROPE, ROPE), bf16),
         ),
         in_specs=[in_vmem] * 6,
-        out_specs=(in_vmem, in_vmem, pl.BlockSpec(memory_space=pltpu.SMEM)),
+        out_specs=(in_vmem, pl.BlockSpec(memory_space=pltpu.SMEM), in_vmem, in_vmem, in_vmem, in_vmem),
         scratch_shapes=scratch,
         name="muon",
         compiler_params=pltpu.CompilerParams(
-            collective_id=0, has_side_effects=True, vmem_limit_bytes=62 * 1024 * 1024
+            collective_id=0, has_side_effects=True, vmem_limit_bytes=VMEM_LIMIT
         ),
-    )(kv_cot.reshape(TOK, 8 * DH2), up_weight, acts, latent, kv_gain.reshape(1, LAT), rope_grad.T)
+    )(kv_cot.reshape(TOK, 8 * DH2), up_weight, acts, latent, kv_gain, rope_grad.T)
+    down, up = pl.pallas_call(
+        finish,
+        out_shape=(shape((COLS, DLOC), bf16), shape((8, LAT, DH2), bf16)),
+        in_specs=[in_vmem] * 5,
+        out_specs=(in_vmem, pl.BlockSpec(memory_space=pl.ANY)),
+        scratch_shapes=[one],
+        name="finish",
+        compiler_params=pltpu.CompilerParams(vmem_limit_bytes=VMEM_LIMIT),
+    )(qm, qc, xall, eall, up)
     return down.T, up, rms.reshape(())
 
 

time: 139 us -> 121 us (0.87)
  Pallas kernels: 124 us -> 115 us
  local copies, waits for them, and re-layouts: 10.2 us -> 2.52 us
    pallas_call x1 -> x2, Pallas kernels: 124 us -> 115 us  [the longest x1 112 us: per_device(): pl.pallas_call(kernel, out_shape=(shape((8, LAT, DH2), bf16), shape((1,),...]
    unnamed x3 -> x11, local copies, waits for them, and re-layouts: 8.9 us -> 2.52 us
where the time goes in v3:
time: 121 us; the launch traced here: 120 us
  Pallas kernels  115 us (95%)
  between operations  2.53 us (2%)
  local copies, waits for them, and re-layouts  2.52 us (2%)
    pallas_call x1, Pallas kernels, per_device(): pl.pallas_call(kernel, out_shape=(shape((8, LAT, DH2), bf16), shape((1,),...  112 us
    unnamed x11, local copies, waits for them, and re-layouts  2.52 us
    pallas_call x1, Pallas kernels, per_device(): pl.pallas_call(finish, out_shape=(shape((COLS, DLOC), bf16), shape((8, LA...  2.45 us

profile of v3, /device:TPU:8, one launch (start us, length us, event | category | flops | bytes accessed | tf_op | source)
XLA Modules:
  0.0 119.8 jit_solution(8059011816155654201)
XLA Ops:
  0.6 0.0 copy-start
  0.6 0.0 copy-start.1
  0.7 0.0 copy-start.2
  0.7 0.0 copy-start.3
  0.7 0.0 copy-start.4
  0.7 2.4 %copy.9 = bf16[64,8,8,256]{3,1,2,0:T(8,128)(2,1)S(1)} copy(bf16[64,8,8,256]{3,2,1,0:T(8,128)(2,1)} %bitcast.7) | data formatting | bytes 4194304
  3.1 0.0 copy-done
  3.1 0.0 copy-done.1
  3.1 0.1 copy-done.2
  3.2 0.0 copy-done.3
  3.2 0.0 copy-done.4
  3.2 112.3 %muon.1 = (bf16[8,512,256]{2,1,0:T(8,128)(2,1)S(1)}, f32[1]{0:T(128)}, bf16[896,512]{1,0:T(8,128)(2,1)S(1)}, bf16[896,128]{1,0:T(8,128)(2,1)S(1)}, bf16[576,512]...) custom-call(bf16[512,2048]{1,0:T(8,128)(2,1)S(1)} %bitcast.5, bf16[8,512,256]{2,1,0:T(8,128)(2,1)S(1)} %copy-done, ...), custom_call_target="tpu_custom_call" | custom-call | tf_op jit(solution)/shard_map/muon/pallas_call | solution.py:490
  115.6 2.4 %finish.1 = (bf16[576,896]{1,0:T(8,128)(2,1)}, bf16[8,512,256]{2,1,0:T(8,128)(2,1)}) custom-call(bf16[576,512]{1,0:T(8,128)(2,1)S(1)} %get-tuple-element.11.qm, bf16[64,64]{1,0:T(8,128)(2,1)S(1)} %get-tuple-element.12.qc, bf16[896,512]{1,0:T(8,128)(2,1)S(1)} %get-tuple-element.13.xall, bf16[896,128]{1,0:T(8,128)(2,1)S(1)} %get-tuple-element.14.eall, ...), custom_call_target="tpu_custom_call" | custom-call | tf_op jit(solution)/shard_map/finish/pallas_call | solution.py:504
Async XLA Ops:
  0.6 2.5 %copy-start = (bf16[8,512,256]{2,1,0:T(8,128)(2,1)S(1)}, bf16[8,512,256]{2,1,0:T(8,128)(2,1)}, u32[]{:S(2)}) copy-start(bf16[8,512,256]{2,1,0:T(8,128)(2,1)} %w.1) | copy-start | bytes 6291460
  0.6 2.5 %copy-start.1 = (bf16[512,896]{1,0:T(8,128)(2,1)S(1)}, bf16[512,896]{1,0:T(8,128)(2,1)}, u32[]{:S(2)}) copy-start(bf16[512,896]{1,0:T(8,128)(2,1)} %acts.1) | copy-start | bytes 2752516
  0.7 2.6 %copy-start.2 = (bf16[512,512]{1,0:T(8,128)(2,1)S(1)}, bf16[512,512]{1,0:T(8,128)(2,1)}, u32[]{:S(2)}) copy-start(bf16[512,512]{1,0:T(8,128)(2,1)} %lat.1) | copy-start | bytes 1572868
  0.7 2.6 %copy-start.3 = (bf16[512,64]{0,1:T(8,128)(2,1)S(1)}, bf16[512,64]{0,1:T(8,128)(2,1)}, u32[]{:S(2)}) copy-start(bf16[512,64]{0,1:T(8,128)(2,1)} %param.11) | copy-start | bytes 196612
  0.7 2.5 %copy-start.4 = (bf16[512]{0:T(512)(128)(2,1)S(1)}, bf16[512]{0:T(512)(128)(2,1)}, u32[]{:S(2)}) copy-start(bf16[512]{0:T(512)(128)(2,1)} %gain.1) | copy-start | bytes 3076

commit v4 on v3

--- a/solution.py
+++ b/solution.py
@@ -28,8 +28,8 @@
 UROWS = LAT // NX
 AROWS, BROWS = 512, 384
 AX, AZ = AROWS // NX, AROWS // (NX * NZ)
-BZ, BX = BROWS // NZ, 16
-UA, UB = 384, 128
+BZ = BROWS // NZ
+UA, UB = 320, 192
 UAX, UBX = UA // NX, UB // NX
 
 VMEM_LIMIT = 40 * 1024 * 1024
@@ -85,26 +85,44 @@
     def prepare(self, value):
         main, corner = value
         rest = jnp.concatenate([main[LAT:, :].T, corner], axis=0)
-        return split(main), split(rest)
+        rest = split(rest)
+        return split(main), rest, jnp.concatenate(rest, axis=1)
+
+    def corner(self, a, b):
+        (main_h, main_l), (rest_h, rest_l), _ = a
+        left = jnp.concatenate([main_h[LAT:], main_l[LAT:]], axis=0)
+        side = jnp.concatenate([rest_h[LAT:], rest_l[LAT:]], axis=0)
+        out = dot(left, b[2][:LAT]) + dot(side, b[2][LAT:])
+        return out[:ROPE, :ROPE] + out[:ROPE, ROPE:] + out[ROPE:, :ROPE]
 
     def product(self, a, b):
-        (main_h, main_l), (rest_h, rest_l) = a
-        (cols_h, cols_l), (tail_h, tail_l) = b
-        rest = jnp.concatenate([rest_h, rest_l, rest_h], axis=1)
-        low_rows = jnp.concatenate([cols_h[LAT:], cols_h[LAT:], cols_l[LAT:]], axis=0)
-        main = dot(main_h, cols_h[:LAT]) + dot(main_h, cols_l[:LAT]) + dot(main_l, cols_h[:LAT])
-        main += dot(rest, low_rows)
-        low_tail = jnp.concatenate([tail_h[LAT:], tail_h[LAT:], tail_l[LAT:]], axis=0)
-        corner = dot(main_h[LAT:], tail_h[:LAT]) + dot(main_h[LAT:], tail_l[:LAT])
-        corner += dot(main_l[LAT:], tail_h[:LAT]) + dot(rest[LAT:], low_tail)
-        return main, corner
+        (main_h, main_l), (rest_h, _), pair = a
+        cols_h, cols_l = b[0]
+        side = jnp.concatenate([pair, rest_h], axis=1)
+        under = jnp.concatenate([cols_h[LAT:], cols_h[LAT:], cols_l[LAT:]], axis=0)
+
+        def block(rows, cols):
+            total = dot(main_h[rows], cols_h[:LAT, cols]) + dot(main_h[rows], cols_l[:LAT, cols])
+            total += dot(main_l[rows], cols_h[:LAT, cols])
+            return total + dot(side[rows], under[:, cols])
+
+        left = block(slice(0, COLS), slice(0, DH2))
+        right = block(slice(DH2, COLS), slice(DH2, LAT))
+        right = jnp.concatenate([left[DH2:LAT].T, right], axis=0)
+        return jnp.concatenate([left, right], axis=1), self.corner(a, b)
 
     def rough(self, a, b):
         main_h, rest_h = a[0][0], a[1][0]
         cols_h, tail_h = b[0][0], b[1][0]
-        main = dot(main_h, cols_h[:LAT]) + dot(rest_h, cols_h[LAT:])
+
+        def block(rows, cols):
+            return dot(main_h[rows], cols_h[:LAT, cols]) + dot(rest_h[rows], cols_h[LAT:, cols])
+
+        left = block(slice(0, COLS), slice(0, DH2))
+        right = block(slice(DH2, COLS), slice(DH2, LAT))
+        right = jnp.concatenate([left[DH2:LAT].T, right], axis=0)
         corner = dot(main_h[LAT:], tail_h[:LAT]) + dot(rest_h[LAT:], tail_h[LAT:])
-        return main, corner
+        return jnp.concatenate([left, right], axis=1), corner
 
 
 class NewtonSchulz:
@@ -135,13 +153,14 @@
         self.store(self.mix, mixed)
         self.advance(parts, self.form.prepare(mixed))
 
-    def middle(self, count):
-        def body(_, carry):
+    def middle(self, count, hook=lambda step: None):
+        def body(step, carry):
+            hook(step)
             parts = self.form.prepare(self.load(self.gram))
             mixed = self.form.prepare(self.mixer(parts))
             self.advance(parts, mixed)
             mix = self.form.prepare(self.load(self.mix))
-            self.store(self.mix, self.form.product(mix, mixed))
+            self.store(self.mix, self.form.rough(mix, mixed) if isinstance(self.form, Large) else self.form.product(mix, mixed))
             return carry
 
         lax.fori_loop(0, count, body, 0)
@@ -156,12 +175,12 @@
 def kernel(
     kv, w, acts, lat, gain, rope, up_out, rms_out, xall, eall, qm_out, qc_out,
     pcs, rcc, csum, ysend, yrecv, comp, acts_t, usend, uxr, uzs, uzr, vzr, vxs, vxr, u,
-    dsend, axr, azs, azr, bzr, bxs, bxr, brow, esend, exr, fsend, frecv, frows,
+    dsend, axr, azs, azr, bzr, bxr, esend, exr, fsend, frecv, frows,
     gpk, gcr, gsum, gyr, gfull, a_main, a_corner, q_main, q_corner, ua_ref, uq_ref,
     s_c, r_c, s_yr, r_yr, s_ya, r_ya, s_ca, r_ca,
     s_ux, r_ux, s_uz, r_uz, s_vz, r_vz, s_vx, r_vx, s_ua, r_ua, s_ub, r_ub, s_oz, r_oz, s_ow, r_ow, s_ox, r_ox,
     s_ax, r_ax, s_az, r_az, s_bz, r_bz, s_bx, r_bx,
-    s_gaz, r_gaz, s_gax, r_gax, s_gbx, r_gbx, s_gbz, r_gbz,
+    s_gaz, r_gaz, s_gax, r_gax, s_gbz, r_gbz,
     s_ex, r_ex, s_ez, r_ez, s_fz, r_fz, s_fx, r_fx,
     s_gc, r_gc, s_gr, r_gr, s_ga, r_ga, s_gb, r_gb,
 ):
@@ -268,6 +287,18 @@
     pl.semaphore_wait(barrier, len(peers))
     first = send(pcs, rcc, s_c, r_c, other)
     csum[...] = cot_rows(c * HALF)
+    lat32 = lat[...].astype(f32)
+    gain32 = gain[...].astype(f32).reshape(1, LAT)
+    inv = lax.rsqrt(jnp.mean(lat32 * lat32, axis=1, keepdims=True) + 1e-06)
+    normed_t = (lat32 * inv * gain32).astype(bf16).T
+    for h in range(8):
+        cols = slice(h * DH2, (h + 1) * DH2)
+        usend[:, cols] = dot(normed_t, kv[:, cols]).astype(bf16)
+
+    u_x = to_all_x(lambda j: usend.at[ds(((x + j) % NX) * UAX, UAX)], lambda j: uxr.at[j - 1], s_ux, r_ux)
+    v_z = to_all_z(
+        lambda j: usend.at[pl.ds(UA, UB), ds(((z + j) % NZ) * DH2, DH2)], lambda j: vzr.at[j - 1], s_vz, r_vz
+    )
     acts_t[...] = acts[...].T
     esend[...] = jnp.concatenate(
         [dot_nt(acts_t[...], rope[...]).astype(bf16), jnp.zeros((DLOC, 128 - ROPE), bf16)], axis=1
@@ -281,18 +312,6 @@
              s_yr.at[j - 1], r_yr.at[j - 1], to_y(j))
         for j in range(1, NY)
     ]
-    lat32 = lat[...].astype(f32)
-    gain32 = gain[...].astype(f32).reshape(1, LAT)
-    inv = lax.rsqrt(jnp.mean(lat32 * lat32, axis=1, keepdims=True) + 1e-06)
-    normed_t = (lat32 * inv * gain32).T.astype(bf16)
-    for h in range(8):
-        cols = slice(h * DH2, (h + 1) * DH2)
-        usend[:, cols] = dot(normed_t, kv[:, cols]).astype(bf16)
-
-    u_x = to_all_x(lambda j: usend.at[ds(((x + j) % NX) * UAX, UAX)], lambda j: uxr.at[j - 1], s_ux, r_ux)
-    v_z = to_all_z(
-        lambda j: usend.at[pl.ds(UA, UB), ds(((z + j) % NZ) * DH2, DH2)], lambda j: vzr.at[j - 1], s_vz, r_vz
-    )
     e_z = scatter_z(sum_x(e_x, esend, exr), fsend, frecv, s_ez, r_ez)
     total = csum[ds(y * QUART, QUART), :]
     for j in range(1, NY):
@@ -327,21 +346,20 @@
     azs[...] = received(a_x, dsend[ds(x * AX, AX), :].astype(f32), axr).astype(bf16)
     a_z = to_all_z(lambda j: azs.at[ds(((z + j) % NZ) * AZ, AZ)], lambda j: azr.at[j - 1], s_az, r_az)
     part = received(b_z, dsend[ds(AROWS + z * BZ, BZ, 16), :].astype(f32), bzr)
-    bxs[0:BZ, :] = part.astype(bf16)
-    bxs[BZ:, :] = jnp.zeros((NX * BX - BZ, LAT), bf16)
-    b_x = to_all_x(lambda j: bxs.at[ds(((x + j) % NX) * BX, BX)], lambda j: bxr.at[j - 1], s_bx, r_bx)
+    bxr[x] = part.astype(bf16)
+    mine_b = bxr.at[x]
+    b_x = to_all_x(lambda j: mine_b, lambda j: mine_b, s_bx, r_bx)
     own = ds(x * AX + z * AZ, AZ)
     xall[own, :] = received(a_z, azs[ds(z * AZ, AZ), :].astype(f32), azr).astype(bf16)
     mine = xall.at[own]
     g_az = to_all_z(lambda j: mine, lambda j: mine, s_gaz, r_gaz)
-    own_b = ds(x * BX, BX)
-    brow[own_b, :] = received(b_x, bxs[own_b, :].astype(f32), bxr).astype(bf16)
-    mine_b = brow.at[own_b]
-    g_bx = to_all_x(lambda j: mine_b, lambda j: mine_b, s_gbx, r_gbx)
-    for copy in g_bx:
-        copy.wait_recv()
+    for copy in b_x:
+        copy.wait_recv()
+    part = bxr[0].astype(f32)
+    for i in range(1, NX):
+        part += bxr[i].astype(f32)
     own_z = ds(AROWS + z * BZ, BZ, 16)
-    xall[own_z, :] = brow[0:BZ, :]
+    xall[own_z, :] = part.astype(bf16)
     mine_z = xall.at[own_z]
     g_bz = to_all_z(lambda j: mine_z, lambda j: mine_z, s_gbz, r_gbz)
     for copy in g_az:
@@ -359,8 +377,8 @@
     u_z = to_all_z(lambda j: uzs.at[(z + j) % NZ], lambda j: uzr.at[j - 1], s_uz, r_uz)
     for copy in g_ax + g_bz + e_ax:
         copy.wait_recv()
-    main_t = [xall[:, i * 128 : (i + 1) * 128].astype(f32).T.astype(bf16) for i in range(4)]
-    tail_t = eall[...].astype(f32).T.astype(bf16)
+    main_t = [xall[:, i * 128 : (i + 1) * 128].T for i in range(4)]
+    tail_t = eall[...].T
     for bi in range(5):
         size = BLOCK_ROWS[bi]
         lhs = main_t[bi] if bi < 4 else tail_t[0:size, :]
@@ -377,7 +395,7 @@
              s_gr.at[j - 1], r_gr.at[j - 1], to_y(j))
         for j in range(1, NY)
     ]
-    rows_a, rows_b = ds(x * UAX, UAX), ds(UA + x * UBX, UBX)
+    rows_a, rows_b = ds(x * UAX, UAX), ds(UA + x * UBX, UBX, 16)
     u[rows_b, :] = received(v_x, vxs[ds(x * UBX, UBX), :].astype(f32), vxr).astype(bf16)
     u_b = to_all_x(lambda j: u.at[rows_b], lambda j: u.at[rows_b], s_ub, r_ub)
     u[rows_a, :] = received(u_z, uzs[z].astype(f32), uzr).astype(bf16)
@@ -385,7 +403,7 @@
     for copy in u_a + u_b:
         copy.wait_recv()
     uval = u[...]
-    ugram = dot(uval.astype(f32).T.astype(bf16), uval)
+    ugram = dot(uval.T, uval)
     usq = jnp.sum(jnp.where(eye(DH2, DH2), ugram, 0.0), keepdims=True)
     unorm = 1.0 / (jnp.sqrt(usq) + 1e-07)
     ua_ref[...] = ugram * unorm * unorm
@@ -405,9 +423,14 @@
     near, far = ds(x * UROWS, UROWS), ds(((x + 2) % NX) * UROWS, UROWS)
     up_out[z, near, :] = dot(u[near, :], uq).astype(bf16)
     up_out[z, far, :] = dot(u[far, :], uq).astype(bf16)
-    o_near, o_far = up_out.at[z, near], up_out.at[z, far]
-    o_z = [send(o_near, o_near, s_oz.at[j - 1], r_oz.at[j - 1], to_z(j)) for j in range(1, NZ)]
-    o_w = [send(o_far, o_far, s_ow.at[j - 1], r_ow.at[j - 1], to_z(j)) for j in range(1, NZ)]
+    half = UROWS // 2
+    parts = [ds(x * UROWS + i * half, half) for i in range(2)]
+    o_z = []
+    for i, rows in enumerate(parts):
+        o_near = up_out.at[z, rows]
+        o_z.append(to_all_z(lambda j: o_near, lambda j: o_near, s_oz.at[i], r_oz.at[i]))
+    o_far = up_out.at[z, far]
+    o_w = to_all_z(lambda j: o_far, lambda j: o_far, s_ow, r_ow)
     for j in range(1, NY):
         g_all[j - 1].wait_recv()
         piece = gfull.at[ds(c * GHALF + ((y - j + NY) % NY) * GQUART, GQUART)]
@@ -432,19 +455,33 @@
             wide = BLOCK_ROWS[bj]
             a_main[bj * 128 : bj * 128 + wide, rows] = block.T[0:wide, :]
     steps = NewtonSchulz(Large(), (a_main, a_corner), (q_main, q_corner))
+    o_x = []
+    for i, rows in enumerate(parts):
+        o_rows = up_out.at[:, rows]
+        o_x.append([
+            pltpu.make_async_remote_copy(
+                src_ref=o_rows, dst_ref=o_rows, send_sem=s_ox.at[i, k], recv_sem=r_ox.at[i, k],
+                device_id=to_x(j), device_id_type=MESH,
+            )
+            for k, j in enumerate((1, 3))
+        ])
+
+    def pass_on(i):
+        for copy in o_z[i]:
+            copy.wait_recv()
+        for copy in o_x[i]:
+            copy.start()
+
+    pass_on(0)
     steps.first()
-    for copy in o_z:
-        copy.wait_recv()
-    o_rows = up_out.at[:, near]
-    o_x = [send(o_rows, o_rows, s_ox.at[i], r_ox.at[i], to_x(j)) for i, j in enumerate((1, 3))]
-    steps.middle(3)
+    steps.middle(3, lambda step: pl.when(step == 1)(lambda: pass_on(1)))
     main, corner = steps.last()
     scale = norm * (0.2 * math.sqrt(D))
     qm_out[...] = (main * scale).astype(bf16)
     qc_out[...] = (corner * scale).astype(bf16)
-    for copy in o_w + o_x:
-        copy.wait_recv()
-    for copy in started:
+    for copy in o_w + o_x[0] + o_x[1]:
+        copy.wait_recv()
+    for copy in started + o_x[0] + o_x[1]:
         copy.wait_send()
 
 
@@ -452,7 +489,7 @@
     store = pltpu.make_async_copy(up, up_out, sem)
     store.start()
     tail = eall[:, 0:ROPE]
-    side = qm[LAT:, :].astype(f32).T.astype(bf16)
+    side = qm[LAT:, :].T
     down_out[0:LAT, :] = (dot_nt(qm[0:LAT, :], xall[...]) + dot_nt(side, tail)).astype(bf16)
     down_out[LAT:, :] = (dot_nt(qm[LAT:, :], xall[...]) + dot_nt(qc[...], tail)).astype(bf16)
     store.wait()
@@ -461,7 +498,7 @@
 def per_device(acts, latent, kv_gain, up_weight, kv_cot, rope_grad):
     vmem = pltpu.VMEM
     one = pltpu.SemaphoreType.DMA
-    sems = lambda n: [pltpu.SemaphoreType.DMA((n,)), pltpu.SemaphoreType.DMA((n,))]
+    sems = lambda *n: [pltpu.SemaphoreType.DMA(n), pltpu.SemaphoreType.DMA(n)]
 
     scratch = [
         vmem((HALF, LAT), bf16), vmem((HALF, LAT), bf16), vmem((HALF, LAT), f32),
@@ -471,8 +508,7 @@
         vmem((7, UAX, DH2), bf16), vmem((7, UB, DH2), bf16), vmem((UB, DH2), bf16),
         vmem((3, UBX, DH2), bf16), vmem((LAT, DH2), bf16),
         vmem((DLOC, LAT), bf16), vmem((3, AX, LAT), bf16), vmem((AX, LAT), bf16), vmem((7, AZ, LAT), bf16),
-        vmem((7, BZ, LAT), bf16), vmem((NX * BX, LAT), bf16), vmem((3, BX, LAT), bf16),
-        vmem((NX * BX, LAT), bf16),
+        vmem((7, BZ, LAT), bf16), vmem((NX, BZ, LAT), bf16),
         vmem((DLOC, 128), bf16), vmem((3, XROWS, 128), bf16), vmem((NZ * ZROWS, 128), bf16),
         vmem((7, ZROWS, 128), bf16), vmem((NZ * ZROWS, 128), bf16),
         vmem((PACKED, 128), f32), vmem((GHALF, 128), f32), vmem((GHALF, 128), f32),
@@ -481,8 +517,8 @@
         vmem((DH2, DH2), f32), vmem((DH2, DH2), f32),
     ]
     scratch += [one, one] + sems(3) + sems(3) + sems(4)
-    scratch += sems(3) + sems(7) + sems(7) + sems(3) + sems(3) + sems(3) + sems(7) + sems(7) + sems(2)
-    scratch += sems(3) + sems(7) + sems(7) + sems(3) + sems(7) + sems(3) + sems(3) + sems(7)
+    scratch += sems(3) + sems(7) + sems(7) + sems(3) + sems(3) + sems(3) + sems(2, 7) + sems(7) + sems(2, 2)
+    scratch += sems(3) + sems(7) + sems(7) + sems(3) + sems(7) + sems(3) + sems(7)
     scratch += sems(3) + sems(7) + sems(7) + sems(3)
     scratch += [one, one] + sems(3) + sems(3) + sems(4)
     in_vmem = pl.BlockSpec(memory_space=pltpu.VMEM)

time: 121 us -> 119 us (0.983)
  Pallas kernels: 115 us -> 112 us
    pallas_call x1, Pallas kernels: 112 us -> 110 us  [per_device(): pl.pallas_call(kernel, out_shape=(shape((8, LAT, DH2), bf16), shape((1,),...]
where the time goes in v4:
time: 119 us; the launch traced here: 117 us
  Pallas kernels  112 us (94%)
  between operations  2.53 us (2%)
  local copies, waits for them, and re-layouts  2.52 us (2%)
    pallas_call x1, Pallas kernels, per_device(): pl.pallas_call(kernel, out_shape=(shape((8, LAT, DH2), bf16), shape((1,),...  110 us
    unnamed x11, local copies, waits for them, and re-layouts  2.52 us
    pallas_call x1, Pallas kernels, per_device(): pl.pallas_call(finish, out_shape=(shape((COLS, DLOC), bf16), shape((8, LA...  2.45 us

profile of v4, /device:TPU:8, one launch (start us, length us, event | category | flops | bytes accessed | tf_op | source)
XLA Modules:
  0.0 117.3 jit_solution(7799060921484227976)
XLA Ops:
  0.6 0.0 copy-start
  0.6 0.0 copy-start.1
  0.7 0.0 copy-start.2
  0.7 0.0 copy-start.3
  0.7 0.0 copy-start.4
  0.7 2.4 %copy.9 = bf16[64,8,8,256]{3,1,2,0:T(8,128)(2,1)S(1)} copy(bf16[64,8,8,256]{3,2,1,0:T(8,128)(2,1)} %bitcast.7) | data formatting | bytes 4194304
  3.1 0.0 copy-done
  3.1 0.0 copy-done.1
  3.1 0.1 copy-done.2
  3.2 0.0 copy-done.3
  3.2 0.0 copy-done.4
  3.2 109.8 %muon.1 = (bf16[8,512,256]{2,1,0:T(8,128)(2,1)S(1)}, f32[1]{0:T(128)}, bf16[896,512]{1,0:T(8,128)(2,1)S(1)}, bf16[896,128]{1,0:T(8,128)(2,1)S(1)}, bf16[576,512]...) custom-call(bf16[512,2048]{1,0:T(8,128)(2,1)S(1)} %bitcast.5, bf16[8,512,256]{2,1,0:T(8,128)(2,1)S(1)} %copy-done, ...), custom_call_target="tpu_custom_call" | custom-call | tf_op jit(solution)/shard_map/muon/pallas_call | solution.py:526
  113.0 2.5 %finish.1 = (bf16[576,896]{1,0:T(8,128)(2,1)}, bf16[8,512,256]{2,1,0:T(8,128)(2,1)}) custom-call(bf16[576,512]{1,0:T(8,128)(2,1)S(1)} %get-tuple-element.11.qm, bf16[64,64]{1,0:T(8,128)(2,1)S(1)} %get-tuple-element.12.qc, bf16[896,512]{1,0:T(8,128)(2,1)S(1)} %get-tuple-element.13.xall, bf16[896,128]{1,0:T(8,128)(2,1)S(1)} %get-tuple-element.14.eall, ...), custom_call_target="tpu_custom_call" | custom-call | tf_op jit(solution)/shard_map/finish/pallas_call | solution.py:540
Async XLA Ops:
  0.6 2.5 %copy-start = (bf16[8,512,256]{2,1,0:T(8,128)(2,1)S(1)}, bf16[8,512,256]{2,1,0:T(8,128)(2,1)}, u32[]{:S(2)}) copy-start(bf16[8,512,256]{2,1,0:T(8,128)(2,1)} %w.1) | copy-start | bytes 6291460
  0.6 2.5 %copy-start.1 = (bf16[512,896]{1,0:T(8,128)(2,1)S(1)}, bf16[512,896]{1,0:T(8,128)(2,1)}, u32[]{:S(2)}) copy-start(bf16[512,896]{1,0:T(8,128)(2,1)} %acts.1) | copy-start | bytes 2752516
  0.7 2.6 %copy-start.2 = (bf16[512,512]{1,0:T(8,128)(2,1)S(1)}, bf16[512,512]{1,0:T(8,128)(2,1)}, u32[]{:S(2)}) copy-start(bf16[512,512]{1,0:T(8,128)(2,1)} %lat.1) | copy-start | bytes 1572868
  0.7 2.6 %copy-start.3 = (bf16[512,64]{0,1:T(8,128)(2,1)S(1)}, bf16[512,64]{0,1:T(8,128)(2,1)}, u32[]{:S(2)}) copy-start(bf16[512,64]{0,1:T(8,128)(2,1)} %param.11) | copy-start | bytes 196612
  0.7 2.5 %copy-start.4 = (bf16[512]{0:T(512)(128)(2,1)S(1)}, bf16[512]{0:T(512)(128)(2,1)}, u32[]{:S(2)}) copy-start(bf16[512]{0:T(512)(128)(2,1)} %gain.1) | copy-start | bytes 3076

commit v5 on v4

--- a/solution.py
+++ b/solution.py
@@ -474,7 +474,7 @@
 
     pass_on(0)
     steps.first()
-    steps.middle(3, lambda step: pl.when(step == 1)(lambda: pass_on(1)))
+    steps.middle(3, lambda step: pl.when(step == 2)(lambda: pass_on(1)))
     main, corner = steps.last()
     scale = norm * (0.2 * math.sqrt(D))
     qm_out[...] = (main * scale).astype(bf16)

time: 119 us -> 120 us (level)
  no operation moved by 1% of the time
where the time goes in v5:
time: 120 us; the launch traced here: 117 us
  Pallas kernels  112 us (93%)
  between operations  2.53 us (2%)
  local copies, waits for them, and re-layouts  2.52 us (2%)
    pallas_call x1, Pallas kernels, per_device(): pl.pallas_call(kernel, out_shape=(shape((8, LAT, DH2), bf16), shape((1,),...  110 us
    unnamed x11, local copies, waits for them, and re-layouts  2.52 us
    pallas_call x1, Pallas kernels, per_device(): pl.pallas_call(finish, out_shape=(shape((COLS, DLOC), bf16), shape((8, LA...  2.45 us

profile of v5, /device:TPU:8, one launch (start us, length us, event | category | flops | bytes accessed | tf_op | source)
XLA Modules:
  0.0 117.3 jit_solution(13045380453736149850)
XLA Ops:
  0.6 0.0 copy-start
  0.6 0.0 copy-start.1
  0.7 0.0 copy-start.2
  0.7 0.0 copy-start.3
  0.7 0.0 copy-start.4
  0.7 2.4 %copy.9 = bf16[64,8,8,256]{3,1,2,0:T(8,128)(2,1)S(1)} copy(bf16[64,8,8,256]{3,2,1,0:T(8,128)(2,1)} %bitcast.7) | data formatting | bytes 4194304
  3.1 0.0 copy-done
  3.1 0.0 copy-done.1
  3.1 0.1 copy-done.2
  3.2 0.0 copy-done.3
  3.2 0.0 copy-done.4
  3.2 109.8 %muon.1 = (bf16[8,512,256]{2,1,0:T(8,128)(2,1)S(1)}, f32[1]{0:T(128)}, bf16[896,512]{1,0:T(8,128)(2,1)S(1)}, bf16[896,128]{1,0:T(8,128)(2,1)S(1)}, bf16[576,512]...) custom-call(bf16[512,2048]{1,0:T(8,128)(2,1)S(1)} %bitcast.5, bf16[8,512,256]{2,1,0:T(8,128)(2,1)S(1)} %copy-done, ...), custom_call_target="tpu_custom_call" | custom-call | tf_op jit(solution)/shard_map/muon/pallas_call | solution.py:526
  113.0 2.5 %finish.1 = (bf16[576,896]{1,0:T(8,128)(2,1)}, bf16[8,512,256]{2,1,0:T(8,128)(2,1)}) custom-call(bf16[576,512]{1,0:T(8,128)(2,1)S(1)} %get-tuple-element.11.qm, bf16[64,64]{1,0:T(8,128)(2,1)S(1)} %get-tuple-element.12.qc, bf16[896,512]{1,0:T(8,128)(2,1)S(1)} %get-tuple-element.13.xall, bf16[896,128]{1,0:T(8,128)(2,1)S(1)} %get-tuple-element.14.eall, ...), custom_call_target="tpu_custom_call" | custom-call | tf_op jit(solution)/shard_map/finish/pallas_call | solution.py:540
Async XLA Ops:
  0.6 2.5 %copy-start = (bf16[8,512,256]{2,1,0:T(8,128)(2,1)S(1)}, bf16[8,512,256]{2,1,0:T(8,128)(2,1)}, u32[]{:S(2)}) copy-start(bf16[8,512,256]{2,1,0:T(8,128)(2,1)} %w.1) | copy-start | bytes 6291460
  0.6 2.5 %copy-start.1 = (bf16[512,896]{1,0:T(8,128)(2,1)S(1)}, bf16[512,896]{1,0:T(8,128)(2,1)}, u32[]{:S(2)}) copy-start(bf16[512,896]{1,0:T(8,128)(2,1)} %acts.1) | copy-start | bytes 2752516
  0.7 2.6 %copy-start.2 = (bf16[512,512]{1,0:T(8,128)(2,1)S(1)}, bf16[512,512]{1,0:T(8,128)(2,1)}, u32[]{:S(2)}) copy-start(bf16[512,512]{1,0:T(8,128)(2,1)} %lat.1) | copy-start | bytes 1572868
  0.7 2.6 %copy-start.3 = (bf16[512,64]{0,1:T(8,128)(2,1)S(1)}, bf16[512,64]{0,1:T(8,128)(2,1)}, u32[]{:S(2)}) copy-start(bf16[512,64]{0,1:T(8,128)(2,1)} %param.11) | copy-start | bytes 196612
  0.7 2.5 %copy-start.4 = (bf16[512]{0:T(512)(128)(2,1)S(1)}, bf16[512]{0:T(512)(128)(2,1)}, u32[]{:S(2)}) copy-start(bf16[512]{0:T(512)(128)(2,1)} %gain.1) | copy-start | bytes 3076
